TPU v7x, 256 devices: a whole 4x4x8 slice. The times are simulated.
256 devices in a mesh: slot: 16 (over y_hi, z), space: 16 (over y_lo, x, core).
Axes of the slice: x: 4, y: 4 (y_hi: 2, y_lo: 2; y = y_hi * 2 + y_lo), z: 8, core: 2. Of those that a mesh axis runs over, the one named last changes fastest.
Arguments:
- queries: bfloat16 [8192, 1024], P('space'), may hold values from -150 to 150
- raw_clip: bfloat16 [8, 32, 64, 2048], P(None, 'space', None, 'slot'), may hold values from -60 to 60
- pool_weight: bfloat16 [27, 2048], P(None, 'slot'), may hold values from -1.25 to 1.25
- old_memory: bfloat16 [16, 4, 16, 32, 2048], P('slot', None, 'space'), may hold values from -6 to 6
- valid_columns: int32 [17], replicated, may hold values from 16 to 32, as said below
- out_weight: bfloat16 [1024, 1024], replicated, may hold values from -0.1875 to 0.1875
Outputs:
- attended: bfloat16 [8192, 1024], P('space')
- fresh_memory: bfloat16 [4, 16, 32, 2048], P(None, 'space', None, 'slot')
- aged_memory: bfloat16 [16, 4, 16, 32, 2048], P('slot', None, 'space')
Inputs may be any that keep to these rules, and one draw needn't show every extreme that they name: `valid_columns`: at least one entry equals 32.
All inputs are finite; a program needn't handle non-finite values.
Results may differ from a plain program's by a relative error of at most 0.0085.
Values may be sent and summed in bfloat16 or wider, within the bound.
A program may use at most 128 MiB of HBM per device.

v0:
```python
from functools import partial

import jax
import jax.numpy as jnp
from jax import lax
from jax.sharding import PartitionSpec as P

H = 16
MC = 32


block_keys = 256
masked_score = -1e30


def from_behind(block, axis, distance):
    devices = range(lax.axis_size(axis))
    route = [(i - distance, i) for i in devices if i - distance in devices]
    return lax.ppermute(block, axis, route)


def combine_parts(first, second):
    peak_first, sum_first, weighted_first = first
    peak_second, sum_second, weighted_second = second
    peak_score = jnp.maximum(peak_first, peak_second)
    factor_first = jnp.exp(peak_first - peak_score)
    factor_second = jnp.exp(peak_second - peak_score)
    weight_sum = sum_first * factor_first + sum_second * factor_second
    weighted = weighted_first * factor_first[..., None] + weighted_second * factor_second[..., None]
    return (peak_score, weight_sum, weighted)


def block_scores(query_heads, memory_rows, first_row, valid_count, head_size):
    key_count = memory_rows.shape[0]
    head_count = query_heads.shape[1]
    unpacked = memory_rows.reshape(key_count, head_count, 2, head_size)
    key_rows = unpacked[:, :, 0, :]
    value_rows = unpacked[:, :, 1, :]
    scores = jnp.einsum(
        "qhd,khd->qhk", query_heads, key_rows, preferred_element_type=jnp.float32
    ) * head_size ** (-0.5)
    column = (first_row + jnp.arange(key_count, dtype=jnp.int32)) % MC
    usable = column < valid_count
    scores = jnp.where(usable[None, None, :], scores, masked_score)
    peak_score = jnp.max(scores, axis=2)
    weights = jnp.where(usable[None, None, :], jnp.exp(scores - peak_score[..., None]), 0.0)
    weight_sum = jnp.sum(weights, axis=2)
    weighted = jnp.einsum(
        "qhk,khd->qhd", weights.astype(jnp.bfloat16), value_rows, preferred_element_type=jnp.float32
    )
    return (peak_score, weight_sum, weighted)


def attend(running, shard_piece, first_row, query_heads, valid_count, head_size):
    key_count = shard_piece.shape[0]
    key_blocks = shard_piece.reshape(key_count // block_keys, block_keys, shard_piece.shape[1])
    offsets = block_keys * jnp.arange(key_count // block_keys, dtype=jnp.int32)

    def advance(state, item_pair):
        key_block, offset = item_pair
        return (
            combine_parts(
                state, block_scores(query_heads, key_block, offset, valid_count, head_size)
            ),
            None,
        )

    return lax.scan(advance, running, (key_blocks, offsets))[0]


def empty_parts(query_rows, head_count, head_size):
    return (
        jnp.full((query_rows, head_count), masked_score, jnp.float32),
        jnp.zeros((query_rows, head_count), jnp.float32),
        jnp.zeros((query_rows, head_count, head_size), jnp.float32),
    )


def pool_slab(raw_clip, pool_weight, head_size):
    upper_row = from_behind(raw_clip[:, -1:], "space", 1)
    stacked = jnp.concatenate([upper_row, raw_clip], axis=1).astype(jnp.float32)
    padded = jnp.pad(stacked, ((1, 0), (0, 0), (1, 0), (0, 0)))
    frames_out = raw_clip.shape[0] // 2
    columns_out = raw_clip.shape[2] // 2
    channels = raw_clip.shape[3]
    weight = pool_weight.astype(jnp.float32)
    pooled = jnp.zeros((frames_out, 1, columns_out, channels), jnp.float32)
    for frame_tap in range(3):
        for row_tap in range(3):
            for column_tap in range(3):
                tapped = padded[
                    frame_tap : frame_tap + 2 * frames_out : 2,
                    row_tap : row_tap + 1,
                    column_tap : column_tap + 2 * columns_out : 2,
                ]
                pooled = pooled + weight[9 * frame_tap + 3 * row_tap + column_tap] * tapped
    shaped = pooled.reshape(frames_out, 1, columns_out, channels // (2 * head_size), 2, head_size)
    center = jnp.mean(shaped, axis=-1, keepdims=True)
    centered = shaped - center
    spread = jnp.mean(centered * centered, axis=-1, keepdims=True)
    normed = centered * lax.rsqrt(spread + 1e-06)
    return normed.reshape(pooled.shape).astype(jnp.bfloat16)


def local(queries, raw_clip, pool_weight, old_memory, valid_columns, out_weight):
    model_width = queries.shape[1]
    head_size = model_width // H
    local_heads = H // lax.axis_size("slot")
    slot_index = lax.axis_index("slot")
    first_head = slot_index * local_heads
    query_rows = queries.shape[0]
    fresh_keys = pool_slab(raw_clip, pool_weight, head_size)
    aged_memory = from_behind(old_memory, "slot", 1)
    query_heads = queries.reshape(query_rows, H, head_size)
    resident = old_memory.reshape(-1, old_memory.shape[-1])
    resident_valid = lax.dynamic_index_in_dim(valid_columns, slot_index + 1, keepdims=False)
    fresh_valid = valid_columns[0]
    fold_slot = partial(
        attend, query_heads=query_heads, valid_count=resident_valid, head_size=head_size
    )
    peak_part, sum_part, weighted_part = fold_slot(
        empty_parts(query_rows, H, head_size),
        lax.all_gather(resident, "space", axis=0, tiled=True),
        jnp.int32(0),
    )
    fresh_rows = fresh_keys.reshape(-1, fresh_keys.shape[-1])
    fresh_queries = lax.dynamic_slice_in_dim(query_heads, first_head, local_heads, axis=1)
    fold_fresh = partial(
        attend, query_heads=fresh_queries, valid_count=fresh_valid, head_size=head_size
    )
    fresh_parts = fold_fresh(
        empty_parts(query_rows, local_heads, head_size),
        lax.all_gather(fresh_rows, "space", axis=0, tiled=True),
        jnp.int32(0),
    )
    window = (
        lax.dynamic_slice_in_dim(peak_part, first_head, local_heads, axis=1),
        lax.dynamic_slice_in_dim(sum_part, first_head, local_heads, axis=1),
        lax.dynamic_slice_in_dim(weighted_part, first_head, local_heads, axis=1),
    )
    joined = combine_parts(window, fresh_parts)
    peak_part = lax.dynamic_update_slice_in_dim(peak_part, joined[0], first_head, axis=1)
    sum_part = lax.dynamic_update_slice_in_dim(sum_part, joined[1], first_head, axis=1)
    weighted_part = lax.dynamic_update_slice_in_dim(weighted_part, joined[2], first_head, axis=1)
    peak_score = lax.pmax(peak_part, "slot")
    factor = jnp.exp(peak_part - peak_score)
    weight_sum, weighted = lax.psum((sum_part * factor, weighted_part * factor[..., None]), "slot")
    mixed_heads = (
        (weighted / weight_sum[..., None]).astype(jnp.bfloat16).reshape(query_rows, model_width)
    )
    attended = jnp.dot(mixed_heads, out_weight, preferred_element_type=jnp.float32).astype(
        jnp.bfloat16
    )
    return (attended, fresh_keys, aged_memory)


def solution(mesh):
    return jax.shard_map(
        local,
        mesh=mesh,
        in_specs=(
            P("space", None),
            P(None, "space", None, "slot"),
            P(None, "slot"),
            P("slot", None, "space", None, None),
            P(),
            P(),
        ),
        out_specs=(
            P("space", None),
            P(None, "space", None, "slot"),
            P("slot", None, "space", None, None),
        ),
        check_vma=False,
    )
```

profile of v0, /device:TPU:32, one launch (start us, length us, event | category | flops | bytes accessed | tf_op | source)
XLA Modules:
  0.0 521.6 jit_solution(1354889459754963036)
XLA Ops:
  8.9 1.7 collective-permute-start
  13.8 2.3 copy.18
  48.8 1.7 multiply_add_fusion
  52.2 21.5 %all_gather.7 = bf16[2048,128]{1,0:T(8,128)(2,1)S(1)} all-gather(bf16[128,128]{1,0:T(8,128)(2,1)S(1)} %bitcast.197), channel_id=1, replica_groups=mesh['slot'=16,'space'=16] {'space'}, dimensions={0}, use_global_device_ids=true | all-gather | bytes 557056 | tf_op jit(solution)/shard_map/all_gather | solution.py:133
  73.6 26.1 %while.35 = (s32[]{:T(128)}, f32[512,1]{0,1:T(1,128)S(1)}, f32[512,1]{0,1:T(1,128)S(1)}, f32[512,1,64]{0,2,1:T(8,128)S(1)}, s32[8]{0:T(128)}, /*index=5*/s32[]{:...) while((s32[]{:T(128)}, f32[512,1]{0,1:T(1,128)S(1)}, ...), condition=%wide.region_9.10_spmd.clone, body=%wide.region_6.9_spmd.clone.sunk | while | flops 34871552 | bytes 2258576 | solution.py:68
  99.8 171.5 %while.34 = (s32[]{:T(128)}, f32[512,16]{0,1:T(8,128)S(1)}, f32[512,16]{0,1:T(8,128)S(1)}, f32[512,16,64]{0,2,1:T(8,128)}, s32[8]{0:T(128)}, /*index=5*/s32[]{:T...) while((s32[]{:T(128)}, f32[512,16]{0,1:T(8,128)S(1)}, ...), condition=%wide.region_3.4_spmd.clone, body=%wide.region_0.3_spmd.clone.sunk | while | flops 566283520 | bytes 73861064 | solution.py:68
  103.5 1.3 copy.28
  104.9 3.3 bitcast_reduce_fusion.2
  108.2 3.2 copy-done.1
  111.4 2.3 fusion.68
  113.7 7.0 %fusion.70 = f32[512,16,64]{0,2,1:T(8,128)} fusion(f32[512,16,64]{0,2,1:T(8,128)} %get-tuple-element.509, f32[16,256,512]{2,1,0:T(8,128)} %copy-done.1, f32[512,16]{0,1:T(8,128)S(1)} %get-tuple-element.477, pred[256]{0:T(512)(128)(4,1)S(1)} %fusion.67, f32[512,16]{0,1:T(8,128)S(1)} %get-tuple-element.480, f32[512,16]{0,1:T(8,128)S(1)} %get-tuple-element.481, ...), kind=kOutput, calls=%fused_computation.11.clone.1 | convolution fusion | flops 281018368 | bytes 13206529 | tf_op jit(solution)/shard_map/while/body/eval_jaxpr/qhk,khd->qhd/dot_general | solution.py:48
  125.8 3.3 bitcast_reduce_fusion.2
  129.1 3.2 copy-done.1
  132.3 2.3 fusion.68
  134.7 7.6 %fusion.70 = f32[512,16,64]{0,2,1:T(8,128)} fusion(f32[512,16,64]{0,2,1:T(8,128)} %get-tuple-element.509, f32[16,256,512]{2,1,0:T(8,128)} %copy-done.1, f32[512,16]{0,1:T(8,128)S(1)} %get-tuple-element.477, pred[256]{0:T(512)(128)(4,1)S(1)} %fusion.67, f32[512,16]{0,1:T(8,128)S(1)} %get-tuple-element.480, f32[512,16]{0,1:T(8,128)S(1)} %get-tuple-element.481, ...), kind=kOutput, calls=%fused_computation.11.clone.1 | convolution fusion | flops 281018368 | bytes 13206529 | tf_op jit(solution)/shard_map/while/body/eval_jaxpr/qhk,khd->qhd/dot_general | solution.py:48
  147.3 3.3 bitcast_reduce_fusion.2
  150.6 3.2 copy-done.1
  153.8 2.3 fusion.68
  156.2 7.6 %fusion.70 = f32[512,16,64]{0,2,1:T(8,128)} fusion(f32[512,16,64]{0,2,1:T(8,128)} %get-tuple-element.509, f32[16,256,512]{2,1,0:T(8,128)} %copy-done.1, f32[512,16]{0,1:T(8,128)S(1)} %get-tuple-element.477, pred[256]{0:T(512)(128)(4,1)S(1)} %fusion.67, f32[512,16]{0,1:T(8,128)S(1)} %get-tuple-element.480, f32[512,16]{0,1:T(8,128)S(1)} %get-tuple-element.481, ...), kind=kOutput, calls=%fused_computation.11.clone.1 | convolution fusion | flops 281018368 | bytes 13206529 | tf_op jit(solution)/shard_map/while/body/eval_jaxpr/qhk,khd->qhd/dot_general | solution.py:48
  168.8 3.3 bitcast_reduce_fusion.2
  172.2 3.2 copy-done.1
  175.4 2.3 fusion.68
  177.7 7.6 %fusion.70 = f32[512,16,64]{0,2,1:T(8,128)} fusion(f32[512,16,64]{0,2,1:T(8,128)} %get-tuple-element.509, f32[16,256,512]{2,1,0:T(8,128)} %copy-done.1, f32[512,16]{0,1:T(8,128)S(1)} %get-tuple-element.477, pred[256]{0:T(512)(128)(4,1)S(1)} %fusion.67, f32[512,16]{0,1:T(8,128)S(1)} %get-tuple-element.480, f32[512,16]{0,1:T(8,128)S(1)} %get-tuple-element.481, ...), kind=kOutput, calls=%fused_computation.11.clone.1 | convolution fusion | flops 281018368 | bytes 13206529 | tf_op jit(solution)/shard_map/while/body/eval_jaxpr/qhk,khd->qhd/dot_general | solution.py:48
  190.3 3.3 bitcast_reduce_fusion.2
  193.7 3.2 copy-done.1
  196.9 2.3 fusion.68
  199.2 7.6 %fusion.70 = f32[512,16,64]{0,2,1:T(8,128)} fusion(f32[512,16,64]{0,2,1:T(8,128)} %get-tuple-element.509, f32[16,256,512]{2,1,0:T(8,128)} %copy-done.1, f32[512,16]{0,1:T(8,128)S(1)} %get-tuple-element.477, pred[256]{0:T(512)(128)(4,1)S(1)} %fusion.67, f32[512,16]{0,1:T(8,128)S(1)} %get-tuple-element.480, f32[512,16]{0,1:T(8,128)S(1)} %get-tuple-element.481, ...), kind=kOutput, calls=%fused_computation.11.clone.1 | convolution fusion | flops 281018368 | bytes 13206529 | tf_op jit(solution)/shard_map/while/body/eval_jaxpr/qhk,khd->qhd/dot_general | solution.py:48
  211.8 3.3 bitcast_reduce_fusion.2
  215.2 3.2 copy-done.1
  218.4 2.3 fusion.68
  220.7 7.6 %fusion.70 = f32[512,16,64]{0,2,1:T(8,128)} fusion(f32[512,16,64]{0,2,1:T(8,128)} %get-tuple-element.509, f32[16,256,512]{2,1,0:T(8,128)} %copy-done.1, f32[512,16]{0,1:T(8,128)S(1)} %get-tuple-element.477, pred[256]{0:T(512)(128)(4,1)S(1)} %fusion.67, f32[512,16]{0,1:T(8,128)S(1)} %get-tuple-element.480, f32[512,16]{0,1:T(8,128)S(1)} %get-tuple-element.481, ...), kind=kOutput, calls=%fused_computation.11.clone.1 | convolution fusion | flops 281018368 | bytes 13206529 | tf_op jit(solution)/shard_map/while/body/eval_jaxpr/qhk,khd->qhd/dot_general | solution.py:48
  233.4 3.3 bitcast_reduce_fusion.2
  236.7 3.2 copy-done.1
  239.9 2.3 fusion.68
  242.2 7.6 %fusion.70 = f32[512,16,64]{0,2,1:T(8,128)} fusion(f32[512,16,64]{0,2,1:T(8,128)} %get-tuple-element.509, f32[16,256,512]{2,1,0:T(8,128)} %copy-done.1, f32[512,16]{0,1:T(8,128)S(1)} %get-tuple-element.477, pred[256]{0:T(512)(128)(4,1)S(1)} %fusion.67, f32[512,16]{0,1:T(8,128)S(1)} %get-tuple-element.480, f32[512,16]{0,1:T(8,128)S(1)} %get-tuple-element.481, ...), kind=kOutput, calls=%fused_computation.11.clone.1 | convolution fusion | flops 281018368 | bytes 13206529 | tf_op jit(solution)/shard_map/while/body/eval_jaxpr/qhk,khd->qhd/dot_general | solution.py:48
  254.9 3.3 bitcast_reduce_fusion.2
  258.2 3.2 copy-done.1
  261.4 2.3 fusion.68
  263.7 7.6 %fusion.70 = f32[512,16,64]{0,2,1:T(8,128)} fusion(f32[512,16,64]{0,2,1:T(8,128)} %get-tuple-element.509, f32[16,256,512]{2,1,0:T(8,128)} %copy-done.1, f32[512,16]{0,1:T(8,128)S(1)} %get-tuple-element.477, pred[256]{0:T(512)(128)(4,1)S(1)} %fusion.67, f32[512,16]{0,1:T(8,128)S(1)} %get-tuple-element.480, f32[512,16]{0,1:T(8,128)S(1)} %get-tuple-element.481, ...), kind=kOutput, calls=%fused_computation.11.clone.1 | convolution fusion | flops 281018368 | bytes 13206529 | tf_op jit(solution)/shard_map/while/body/eval_jaxpr/qhk,khd->qhd/dot_general | solution.py:48
  271.5 74.1 %pmax.7 = f32[512,16]{0,1:T(8,128)S(1)} all-reduce(f32[512,16]{0,1:T(8,128)S(1)} %dynamic_update_slice.10), channel_id=1, replica_groups=mesh['slot'=16,'space'=16] {'slot'}, use_global_device_ids=true, to_apply=%region_10.11 | all-reduce | flops 8192 | bytes 65536 | tf_op jit(solution)/shard_map/pmax | solution.py:145
  345.6 1.6 add_dynamic-update-slice_fusion
  347.2 3.2 broadcast_multiply_fusion
  351.4 4.2 collective-permute-start.1
  355.6 11.1 %collective-permute-done.1 = bf16[1,4,1,32,2048]{4,3,2,1,0:T(8,128)(2,1)S(1)} collective-permute-done((bf16[1,4,1,32,2048]{4,3,2,1,0:T(8,128)(2,1)S(1)}, bf16[1,4,1,32,2048]{4,3,2,1,0:T(8,128)(2,1)S(1)}, u32[]{:S(2)}, u32[]{:S(2)}) %collective-permute-start.1) | collective-permute-done | bytes 524320 | tf_op jit(solution)/shard_map/ppermute | solution.py:19
  366.7 69.2 %psum.15 = f32[512,16]{0,1:T(8,128)S(1)} all-reduce(f32[512,16]{0,1:T(8,128)S(1)} %get-tuple-element.335), channel_id=1, replica_groups=mesh['slot'=16,'space'=16] {'slot'}, use_global_device_ids=true, to_apply=%region_12.13 | all-reduce | flops 8192 | bytes 65536 | tf_op jit(solution)/shard_map/psum | solution.py:147
  435.9 73.9 %all-reduce.3.cloned.1.call-done = f32[512,16,64]{0,2,1:T(8,128)} async-done(((f32[512,16,64]{0,2,1:T(8,128)}), f32[512,16,64]{0,2,1:T(8,128)}) %all-reduce.3.cloned.1.call-update) | async-done | bytes 2097168 | tf_op jit(solution)/shard_map/psum | solution.py:147
  509.8 1.9 divide_convert_fusion
  511.7 2.3 convolution_convert_fusion
  (196 shorter events, 106.4 us)
Async XLA Ops:
  7.2 504.5 %copy-start = (bf16[1024,1024]{1,0:T(8,128)(2,1)S(1)}, bf16[1024,1024]{1,0:T(8,128)(2,1)}, u32[]{:S(2)}) copy-start(bf16[1024,1024]{1,0:T(8,128)(2,1)} %param.15) | copy-start | bytes 6291460
  7.2 92.6 %all-gather.2.cloned.1.call-start = ((), (), s32[]{:S(2)}) async-start(), calls=%async_computation | async-start | bytes 8912896 | tf_op jit(solution)/shard_map/all_gather | solution.py:123
  7.9 501.9 %all-reduce.3.cloned.1.call-start = ((), (), s32[]{:S(2)}) async-start(), calls=%async_computation.1 | async-start | bytes 4194304 | tf_op jit(solution)/shard_map/psum | solution.py:147
  8.9 8.0 %collective-permute-start = (bf16[8,1,64,128]{3,2,1,0:T(8,128)(2,1)S(1)}, bf16[8,1,64,128]{3,2,1,0:T(8,128)(2,1)S(1)}, u32[]{:S(2)}, u32[]{:S(2)}) collective-permute-start(bf16[8,1,64,128]{3,2,1,0:T(8,128)(2,1)S(1)} %slice.194), channel_id=1, source_target_pairs={{0,1},{1,2},{2,3},{3,4},{4,5},{5,6},{6,7},{7,8},{8,9},{9,10},{10,1... | collective-permute-start | bytes 393224 | tf_op jit(solution)/shard_map/ppermute | solution.py:19
  52.2 21.5 %copy-start.4 = (bf16[4,1,32,128]{3,2,1,0:T(8,128)(2,1)}, bf16[4,1,32,128]{3,2,1,0:T(8,128)(2,1)S(1)}, u32[]{:S(2)}) copy-start(bf16[4,1,32,128]{3,2,1,0:T(8,128)(2,1)S(1)} %multiply_convert_fusion) | copy-start | bytes 98308
  108.2 3.2 copy-start.1
  111.4 2.3 copy-start.2
  129.1 3.2 copy-start.1
  132.3 2.3 copy-start.2
  150.6 3.2 copy-start.1
  153.8 2.3 copy-start.2
  172.2 3.2 copy-start.1
  175.4 2.3 copy-start.2
  193.7 3.2 copy-start.1
  196.9 2.3 copy-start.2
  215.2 3.2 copy-start.1
  218.4 2.3 copy-start.2
  236.7 3.2 copy-start.1
  239.9 2.3 copy-start.2
  258.2 3.2 copy-start.1
  261.4 2.3 copy-start.2
  350.4 1.0 copy-start.3
  351.4 15.3 %collective-permute-start.1 = (bf16[1,4,1,32,2048]{4,3,2,1,0:T(8,128)(2,1)S(1)}, bf16[1,4,1,32,2048]{4,3,2,1,0:T(8,128)(2,1)S(1)}, u32[]{:S(2)}, u32[]{:S(2)}) collective-permute-start(bf16[1,4,1,32,2048]{4,3,2,1,0:T(8,128)(2,1)S(1)} %copy-done.3), channel_id=1, source_target_pairs={{0,16},{16,32},{32,48},{48,64},{64,80},{80,96},{96,112},{112,128},... | collective-permute-start | bytes 1572872 | tf_op jit(solution)/shard_map/ppermute | solution.py:19
Sparse Core Ops, SparseCore 0:
  9.8 59.1 all-gather.1
  350.5 159.2 all-reduce.2
where the time goes:
time: 524 us; the launch traced here: 522 us
  blocking collectives  165 us (31%)
  local copies, waits for them, and re-layouts  106 us (20%)
  matrix products  93 us (18%)
  waiting for transfers between devices  85.7 us (16%)
  other arithmetic  51.2 us (10%)
  between operations  14.2 us (3%)
  starting transfers between devices  6.04 us (1%)
    pmax x1, blocking collectives, local(): peak_score = lax.pmax(peak_part, 'slot')  74.1 us
    psum x1, waiting for transfers between devices, local(): lax.psum((sum_part * factor, weighted_part * factor[..., None]), 'slot')  73.9 us
    psum x1, blocking collectives, local(): lax.psum((sum_part * factor, weighted_part * factor[..., None]), 'slot')  69.2 us
    dot_general x16, matrix products, block_scores(): jnp.einsum('qhk,khd->qhd', weights.astype(jnp.bfloat16), value_rows, pref...  62 us
    dynamic_slice x48, local copies, waits for them, and re-layouts, attend(): return lax.scan(advance, running, (key_blocks, offsets))[0]  40.5 us
    slice x27, local copies, waits for them, and re-layouts, pool_slab(): padded[frame_tap:frame_tap + 2 * frames_out:2, row_tap:row_tap + 1, colum...  30.9 us
    dot_general x16, matrix products, block_scores(): jnp.einsum('qhd,khd->qhk', query_heads, key_rows, preferred_element_type=...  28.7 us
    while x32, local copies, waits for them, and re-layouts  25.7 us
  transfers between devices with their start and end apart: 4, of which 2 were waited for; matrix products, arithmetic and copies ran while one was open for 13% of the time, Pallas kernels for 0%

commit v1 on v0

v1 whole, which is shorter than its diff:
```python
import math

import jax
import jax.numpy as jnp
from jax import lax
from jax.experimental import pallas as pl
from jax.experimental.pallas import tpu as pltpu
from jax.sharding import PartitionSpec as P

F32 = jnp.float32
BF16 = jnp.bfloat16
MESH = pl.DeviceIdType.MESH
N = 16
HD = 64
TOK = 128
QB = 512
NK = (N + 1) * TOK
TQ = 256
MC = 32
MASKED = -1e30
PAIRS = N // 2
OWN = QB // N
RING = 8


def to(slot, space):
    return {"slot": slot, "space": space}


def remote(src, dst, send, recv, slot, space):
    return pltpu.make_async_remote_copy(
        src_ref=src, dst_ref=dst, send_sem=send, recv_sem=recv, device_id=to(slot, space), device_id_type=MESH
    )


def wait_bytes(ref, sem):
    pltpu.make_async_copy(ref, ref, sem).wait()


def kernel(
    q_hbm, raw_hbm, pw_ref, old_hbm, valid, w_hbm,
    out, fresh, aged,
    qv, qt, qall, kv, kaug, vt, S, qa, ot, lt, sb, rb, ls, lr, mx, mr, att, sel, wv, rawv, halo, xf, zeros,
    lsem, lsem2, lsem3, lsem4, lsem5,
    halo_s, halo_r, kv_s, kv_r, q_s, q_r, fr_s, fr_r, ag_s, ag_r, res_s, res_r, lse_s, lse_r, mx_s, mx_r, at_s, at_r,
):
    s = lax.axis_index("slot")
    p = lax.axis_index("space")
    lane = lambda shape: lax.broadcasted_iota(jnp.int32, shape, 1)

    q_copy = pltpu.make_async_copy(q_hbm, qv, lsem)
    q_copy.start()
    raw_copy = pltpu.make_async_copy(raw_hbm, rawv, lsem2)
    raw_copy.start()
    kv_copy = pltpu.make_async_copy(
        old_hbm.at[:, pl.ds(pl.multiple_of(p * TOK, TOK), TOK)], kv.at[p], lsem3
    )
    kv_copy.start()
    w_copy = pltpu.make_async_copy(w_hbm, wv, lsem4)
    w_copy.start()

    barrier = pltpu.get_barrier_semaphore()
    for d in range(1, N):
        pl.semaphore_signal(barrier, inc=1, device_id=to(s, lax.rem(p + d, N)), device_id_type=MESH)
    for d in range(1, N):
        pl.semaphore_signal(barrier, inc=1, device_id=to(lax.rem(s + d, N), p), device_id_type=MESH)

    @pl.when(s != p)
    def _():
        pl.semaphore_signal(barrier, inc=1, device_id=to(p, s), device_id_type=MESH)

    q_copy.wait()
    for c in range(PAIRS):
        qt[c * 128 : (c + 1) * 128, :] = qv[:, c * 128 : (c + 1) * 128].T

    row_i = lax.broadcasted_iota(jnp.int32, (256, N * HD), 0)
    col_i = lax.broadcasted_iota(jnp.int32, (256, N * HD), 1)
    sel[...] = jnp.where(row_i % 128 == col_i // HD, 1.0, 0.0).astype(BF16)
    ones_row = jnp.where(lax.broadcasted_iota(jnp.int32, (HD, TQ), 0) == 0, 1.0, 0.0).astype(BF16)
    for a in range(2):
        for t in range(4):
            qa[a, t, 3 * HD :, :] = ones_row

    @pl.when(s != p)
    def _():
        pl.semaphore_wait(barrier, 2 * (N - 1) + 1)

    @pl.when(s == p)
    def _():
        pl.semaphore_wait(barrier, 2 * (N - 1))

    @pl.when(p < N - 1)
    def _():
        remote(raw_hbm.at[:, 1], halo, halo_s, halo_r, s, p + 1).start()

    for d in range(1, N):
        peer = lax.rem(p + d, N)
        remote(
            old_hbm.at[:, pl.ds(pl.multiple_of(peer * TOK, TOK), TOK)], kv.at[p], kv_s, kv_r, s, peer
        ).start()
    for d in range(1, N):
        peer = lax.rem(p + d, N)
        remote(
            qt.at[pl.ds(pl.multiple_of(peer * HD, HD), HD), :], qall.at[p], q_s, q_r.at[p], s, peer
        ).start()

    @pl.when(s < N - 1)
    def _():
        remote(old_hbm, aged, ag_s, ag_r, s + 1, p).start()

    @pl.when(s == 0)
    def _():
        zeros[...] = jnp.zeros_like(zeros)
        pltpu.make_async_copy(zeros, aged, lsem5).start()

    raw_copy.wait()

    @pl.when(p > 0)
    def _():
        wait_bytes(halo, halo_r)

    @pl.when(p == 0)
    def _():
        halo[...] = jnp.zeros_like(halo)

    edge = jnp.zeros((8, 8, 128), F32)
    for b in range(3):
        xf[b, :, 0:8, :] = edge
        xf[b, :, 8:, :] = (halo[...] if b == 0 else rawv[:, b - 1]).astype(F32)
    weight = pw_ref[...].astype(F32)
    half = lane((MC, 128)) < HD
    for f in range(4):
        total = jnp.zeros((MC, 128), F32)
        for a in range(3):
            frame = 2 * f + a - 1
            if frame < 0:
                continue
            for b in range(3):
                for g in range(3):
                    tap = 9 * a + 3 * b + g
                    total += weight[tap : tap + 1, :] * xf[b, frame, pl.ds(7 + g, MC, stride=2), :]
        mean_lo = jnp.sum(jnp.where(half, total, 0.0), axis=1, keepdims=True) / HD
        mean_hi = jnp.sum(jnp.where(half, 0.0, total), axis=1, keepdims=True) / HD
        centred = total - jnp.where(half, mean_lo, mean_hi)
        square = centred * centred
        var_lo = jnp.sum(jnp.where(half, square, 0.0), axis=1, keepdims=True) / HD
        var_hi = jnp.sum(jnp.where(half, 0.0, square), axis=1, keepdims=True) / HD
        normed = centred * lax.rsqrt(jnp.where(half, var_lo, var_hi) + 1e-06)
        fresh[f * MC : (f + 1) * MC, :] = normed.astype(BF16)

    @pl.when(s != p)
    def _():
        remote(fresh, kv.at[N], fr_s, fr_r, p, s).start()

    @pl.when(s == p)
    def _():
        kv[N] = fresh[...]

    qall[p] = qt[pl.ds(pl.multiple_of(p * HD, HD), HD), :]

    def prepare(i, count):
        x = kv[i].astype(F32)
        turned = pltpu.roll(x, HD, 1)
        low = lane((TOK, TOK)) < HD
        column = lax.broadcasted_iota(jnp.int32, (TOK, TOK), 0) % MC
        mask = jnp.where((lane((TOK, TOK)) == HD) & (column >= count), MASKED, 0.0)
        row = pl.ds(pl.multiple_of(i * TOK, TOK), TOK)
        kaug[row, 0:128] = jnp.where(low, x, turned).astype(BF16)
        kaug[row, 128:256] = jnp.where(low, x, mask).astype(BF16)
        upper = lax.broadcasted_iota(jnp.int32, (TOK, TOK), 0) < HD
        vt[:, row] = jnp.where(upper, 1.0, x.T).astype(BF16)

    kv_copy.wait()
    wait_bytes(kv.at[pl.ds(0, N - 1)], kv_r)
    own_count = valid[s + 1]
    fresh_count = valid[0]

    def prepare_old(i, carry):
        prepare(i, own_count)
        return carry

    lax.fori_loop(0, N, prepare_old, 0)

    @pl.when(s != p)
    def _():
        wait_bytes(kv.at[N], fr_r)

    prepare(N, fresh_count)

    scale = HD ** (-0.5) * math.log2(math.e)
    pair0 = p // 2

    def pair_of(i):
        return lax.rem(pair0 - i + PAIRS, PAIRS)

    def build(i):
        pair = pair_of(i)
        a = i % 2
        for b in range(2):
            for h in range(2):
                x = qall[2 * pair + b, :, h * TQ : (h + 1) * TQ].astype(F32) * scale
                first = x.astype(BF16)
                x = x - first.astype(F32)
                second = x.astype(BF16)
                x = x - second.astype(F32)
                t = 2 * b + h
                qa[a, t, 0:HD, :] = first
                qa[a, t, HD : 2 * HD, :] = second
                qa[a, t, 2 * HD : 3 * HD, :] = x.astype(BF16)

    def scores(a, t, z):
        peak = None
        for c in range(0, NK, 128):
            block = jnp.dot(kaug[c : c + 128, :], qa[a, t], preferred_element_type=F32)
            S[z, c : c + 128, :] = block
            top = jnp.max(block.reshape(16, 8, TQ), axis=0)
            peak = top if peak is None else jnp.maximum(peak, top)
        return peak

    def weigh(pair, t, z, peak):
        top = jnp.max(peak, axis=0, keepdims=True)
        total = None
        for c in range(0, NK, 256):
            n = min(256, NK - c)
            weights = jnp.exp2(S[z, c : c + n, :] - top).astype(BF16)
            part = jnp.dot(vt[:, c : c + n], weights, preferred_element_type=F32)
            total = part if total is None else total + part
        b, h = t // 2, t % 2
        ot[b * HD : (b + 1) * HD, h * TQ : (h + 1) * TQ] = total[HD:, :] / total[:HD, :]
        lt[pl.ds(2 * pair + b, 1), h * TQ : (h + 1) * TQ] = top + jnp.log2(total[0:1, :])

    wait_bytes(qall.at[0], q_r.at[p + 1 - 2 * lax.rem(p, 2)])
    build(0)
    first_peak = scores(0, 0, 0)

    def step(i, peak):
        pair = pair_of(i)

        @pl.when(i < PAIRS - 1)
        def _():
            coming = pair_of(i + 1)
            wait_bytes(qall.at[0], q_r.at[2 * coming])
            wait_bytes(qall.at[0], q_r.at[2 * coming + 1])

        build(i + 1)
        for t in range(4):
            if t < 3:
                later = scores(i % 2, t + 1, (t + 1) % 2)
            else:
                later = scores((i + 1) % 2, 0, 0)
            weigh(pair, t, t % 2, peak)
            peak = later
        sb[pair] = ot[...].T.astype(BF16).reshape(N, OWN, 128)
        for d in range(1, N):
            owner = lax.rem(s + d, N)
            remote(sb.at[pair, owner], rb.at[s, pair], res_s, res_r, owner, p).start()
        return peak

    lax.fori_loop(0, PAIRS, step, first_peak)

    lse = lt[...]
    first = lse.astype(BF16).astype(F32)
    second = (lse - first).astype(BF16).astype(F32)
    third = lse - first - second
    stacked = jnp.concatenate([first, second, third, jnp.zeros((128 - 3 * N, QB), F32)], axis=0)
    ls[...] = stacked.T.astype(BF16).reshape(N, OWN, 128)
    for d in range(1, N):
        owner = lax.rem(s + d, N)
        remote(ls.at[owner], lr.at[s], lse_s, lse_r, owner, p).start()
    lr[s] = ls[s]
    rb[s] = sb[:, s]

    wait_bytes(lr.at[pl.ds(0, N - 1)], lse_r)
    parts = lr[...].astype(F32).reshape(N * OWN, 128)
    parts = parts + pltpu.roll(parts, 128 - N, 1) + pltpu.roll(parts, 128 - 2 * N, 1)
    parts = jnp.where(lane((N * OWN, 128)) < N, parts, 0.0).reshape(N, OWN, 128)
    share = jnp.exp2(parts - jnp.max(parts, axis=0, keepdims=True))
    share = (share / jnp.sum(share, axis=0, keepdims=True)).reshape(N * OWN, 128)
    share_hi = share.astype(BF16)
    share_lo = (share - share_hi.astype(F32)).astype(BF16)
    shares = jnp.concatenate([share_hi, share_lo], axis=1)
    wait_bytes(rb.at[pl.ds(0, N - 1)], res_r)
    for j in range(PAIRS):
        spread = jnp.dot(shares, sel[:, j * 128 : (j + 1) * 128], preferred_element_type=F32)
        mixed = jnp.sum(spread.reshape(N, OWN, 128) * rb[:, j].astype(F32), axis=0)
        mx[j] = mixed.astype(BF16)

    for d in range(1, N):
        peer = lax.rem(p + d, N)
        remote(mx.at[peer // 2], mr.at[p], mx_s, mx_r, s, peer).start()
    mr[p] = mx[p // 2]
    w_copy.wait()
    wait_bytes(mr.at[pl.ds(0, N - 1)], mx_r)
    odd = lax.rem(p, 2) == 1
    left = lane((OWN, 128)) < HD
    pieces = []
    for j in range(PAIRS):
        a = mr[2 * j].astype(F32)
        b = mr[2 * j + 1].astype(F32)
        a = jnp.where(odd, pltpu.roll(a, HD, 1), a)
        b = jnp.where(odd, b, pltpu.roll(b, HD, 1))
        pieces.append(jnp.where(left, a, b).astype(BF16))
    heads = jnp.concatenate(pieces, axis=1)
    att[...] = jnp.dot(heads, wv[...], preferred_element_type=F32).astype(BF16)

    y, z = s // RING, lax.rem(s, RING)

    def rows(index):
        return out.at[pl.ds(pl.multiple_of(index * OWN, OWN), OWN), :]

    def near(dz):
        return y * RING + lax.rem(z + dz + RING, RING)

    def far(dz):
        return (1 - y) * RING + lax.rem(z + dz + RING, RING)

    def give(index, target, src=None, count=0):
        remote(rows(index) if src is None else src, rows(index), at_s.at[count], at_r.at[index], target, p).start()

    def got(index):
        wait_bytes(rows(0), at_r.at[index])

    sent = [0]

    def push(index, target, src=None):
        give(index, target, src, sent[0])
        sent[0] += 1

    push(s, far(0), att)
    push(s, near(1), att)
    push(s, near(-1), att)
    out[pl.ds(pl.multiple_of(s * OWN, OWN), OWN), :] = att[...]
    got(far(0))
    push(far(0), near(1))
    push(far(0), near(-1))
    for k in range(1, 4):
        got(near(-k))
        push(near(-k), near(1))
        got(near(k))
        if k < 3:
            push(near(k), near(-1))
        got(far(-k))
        if k < 3:
            push(far(-k), near(1))
        got(far(k))
        push(far(k), near(-1))
    got(near(-4))
    got(far(4))

    for i in range(sent[0]):
        wait_bytes(rows(0), at_s.at[i])
    wait_bytes(kv.at[pl.ds(0, N - 1)], kv_s)
    wait_bytes(qall.at[pl.ds(0, N - 1)], q_s)
    wait_bytes(rb.at[pl.ds(0, N - 1)], res_s)
    wait_bytes(lr.at[pl.ds(0, N - 1)], lse_s)
    wait_bytes(mr.at[pl.ds(0, N - 1)], mx_s)

    @pl.when(p < N - 1)
    def _():
        wait_bytes(halo, halo_s)

    @pl.when(s != p)
    def _():
        wait_bytes(kv.at[N], fr_s)

    @pl.when(s < N - 1)
    def _():
        wait_bytes(old_hbm, ag_s)

    @pl.when(s > 0)
    def _():
        wait_bytes(old_hbm, ag_r)

    @pl.when(s == 0)
    def _():
        pltpu.make_async_copy(zeros, aged, lsem5).wait()


def local(queries, raw_clip, pool_weight, old_memory, valid_columns, out_weight):
    dma = pltpu.SemaphoreType.DMA
    anywhere = pl.BlockSpec(memory_space=pl.ANY)
    vmem = pl.BlockSpec(memory_space=pltpu.VMEM)
    attended, fresh, aged = pl.pallas_call(
        kernel,
        out_shape=(
            jax.ShapeDtypeStruct((QB, N * HD), BF16),
            jax.ShapeDtypeStruct((TOK, TOK), BF16),
            jax.ShapeDtypeStruct((TOK, N * TOK), BF16),
        ),
        in_specs=[anywhere, anywhere, vmem, anywhere, pl.BlockSpec(memory_space=pltpu.SMEM), anywhere],
        out_specs=(vmem, vmem, anywhere),
        scratch_shapes=[
            pltpu.VMEM((QB, N * HD), BF16),
            pltpu.VMEM((N * HD, QB), BF16),
            pltpu.VMEM((N, HD, QB), BF16),
            pltpu.VMEM((N + 1, TOK, TOK), BF16),
            pltpu.VMEM((NK, 256), BF16),
            pltpu.VMEM((128, NK), BF16),
            pltpu.VMEM((2, NK, TQ), F32),
            pltpu.VMEM((2, 4, 256, TQ), BF16),
            pltpu.VMEM((128, QB), F32),
            pltpu.VMEM((N, QB), F32),
            pltpu.VMEM((PAIRS, N, OWN, 128), BF16),
            pltpu.VMEM((N, PAIRS, OWN, 128), BF16),
            pltpu.VMEM((N, OWN, 128), BF16),
            pltpu.VMEM((N, OWN, 128), BF16),
            pltpu.VMEM((PAIRS, OWN, 128), BF16),
            pltpu.VMEM((N, OWN, 128), BF16),
            pltpu.VMEM((OWN, N * HD), BF16),
            pltpu.VMEM((256, N * HD), BF16),
            pltpu.VMEM((N * HD, N * HD), BF16),
            pltpu.VMEM((8, 2, 64, 128), BF16),
            pltpu.VMEM((8, 64, 128), BF16),
            pltpu.VMEM((3, 8, 72, 128), F32),
            pltpu.VMEM((TOK, N * TOK), BF16),
            dma, dma, dma, dma, dma,
            dma, dma, dma, dma, dma, dma((N,)), dma, dma, dma, dma, dma, dma, dma, dma, dma, dma, dma((16,)), dma((N,)),
        ],
        compiler_params=pltpu.CompilerParams(
            collective_id=0, has_side_effects=True, vmem_limit_bytes=48 << 20
        ),
        name="attend",
    )(
        queries,
        raw_clip,
        pool_weight,
        old_memory.reshape(TOK, N * TOK),
        valid_columns,
        out_weight,
    )
    return (attended, fresh.reshape(4, 1, MC, TOK), aged.reshape(old_memory.shape))


def solution(mesh):
    return jax.shard_map(
        local,
        mesh=mesh,
        in_specs=(
            P("space", None),
            P(None, "space", None, "slot"),
            P(None, "slot"),
            P("slot", None, "space", None, None),
            P(),
            P(),
        ),
        out_specs=(
            P("space", None),
            P(None, "space", None, "slot"),
            P("slot", None, "space", None, None),
        ),
        check_vma=False,
    )
```

time: 524 us -> 109 us (0.21)
  blocking collectives: 165 us -> 0 us
  Pallas kernels: 0 us -> 98 us
  local copies, waits for them, and re-layouts: 106 us -> 8.53 us
  matrix products: 93 us -> 0 us
  waiting for transfers between devices: 85.7 us -> 0 us
  other arithmetic: 51.2 us -> 0 us
  between operations: 14.2 us -> 0.65 us
  starting transfers between devices: 6.04 us -> 0 us
    pallas_call x0 -> x1, Pallas kernels: none -> 98 us  [local(): pl.pallas_call(kernel, out_shape=(jax.ShapeDtypeStruct((QB, N * HD), BF16...]
    dot_general x33 -> x0, matrix products: 93 us -> none  [the longest x16 62 us: block_scores(): jnp.einsum('qhk,khd->qhd', weights.astype(jnp.bfloat16), value_rows, pref...]
    pmax x1 -> x0, blocking collectives: 74.1 us -> none  [local(): peak_score = lax.pmax(peak_part, 'slot')]
    psum x1 -> x0, waiting for transfers between devices: 73.9 us -> none  [local(): lax.psum((sum_part * factor, weighted_part * factor[..., None]), 'slot')]
    psum x1 -> x0, blocking collectives: 69.2 us -> none  [local(): lax.psum((sum_part * factor, weighted_part * factor[..., None]), 'slot')]
    dynamic_slice x49 -> x0, local copies, waits for them, and re-layouts: 41.4 us -> none  [the longest x48 40.5 us: attend(): return lax.scan(advance, running, (key_blocks, offsets))[0]]
    slice x29 -> x0, local copies, waits for them, and re-layouts: 33.1 us -> none  [the longest x27 30.9 us: pool_slab(): padded[frame_tap:frame_tap + 2 * frames_out:2, row_tap:row_tap + 1, colum...]
    while x32 -> x0, local copies, waits for them, and re-layouts: 25.7 us -> none
  transfers between devices with their start and end apart: 4 -> 0, of which waited for: 2 -> 0; matrix products, arithmetic and copies ran while one was open for 13% -> 0% of each run, Pallas kernels for 0% -> 0%
where the time goes in v1:
time: 109 us; the launch traced here: 107 us
  Pallas kernels  98 us (90%)
  local copies, waits for them, and re-layouts  8.53 us (8%)
    pallas_call x1, Pallas kernels, local(): pl.pallas_call(kernel, out_shape=(jax.ShapeDtypeStruct((QB, N * HD), BF16...  98 us
    unnamed x15, local copies, waits for them, and re-layouts  8.53 us

profile of v1, /device:TPU:32, one launch (start us, length us, event | category | flops | bytes accessed | tf_op | source)
XLA Modules:
  0.0 107.2 jit_solution(16694905477793794418)
XLA Ops:
  0.6 0.0 copy-start
  0.6 1.6 %copy-done = bf16[1024,1024]{1,0:T(8,128)(2,1)S(1)} copy-done((bf16[1024,1024]{1,0:T(8,128)(2,1)S(1)}, bf16[1024,1024]{1,0:T(8,128)(2,1)}, u32[]{:S(2)}) %copy-start) | copy-done | bytes 2097176
  2.2 0.0 copy-start.1
  2.2 1.2 %copy-done.1 = bf16[512,1024]{1,0:T(8,128)(2,1)S(1)} copy-done((bf16[512,1024]{1,0:T(8,128)(2,1)S(1)}, bf16[512,1024]{1,0:T(8,128)(2,1)}, u32[]{:S(2)}) %copy-start.1) | copy-done | bytes 1048600
  3.4 0.0 copy-start.2
  3.5 1.0 copy-done.2
  4.5 0.0 copy-start.3
  4.5 0.9 copy-done.3
  5.4 0.0 copy-start.4
  5.4 0.7 copy-done.4
  6.1 0.0 copy-start.5
  6.1 0.7 copy-done.5
  6.8 98.0 %attend.1 = (bf16[512,1024]{1,0:T(8,128)(2,1)S(1)}, bf16[128,128]{1,0:T(8,128)(2,1)S(1)}, bf16[128,2048]{1,0:T(8,128)(2,1)S(1)}) custom-call(bf16[512,1024]{1,0:T(8,128)(2,1)S(1)} %copy-done.1, bf16[8,2,64,128]{3,2,1,0:T(8,128)(2,1)S(1)} %copy-done.3, bf16[27,128]{1,0:T(8,128)(2,1)S(1)} %copy-done.4, bf16[128,2048]{1,0:T(8,128)(2,1)S(1)} %bitcast.7, ...), custom_call_target="tpu_custom_call" | custom-call | tf_op jit(solution)/shard_map/attend/pallas_call | solution.py:383
  104.8 1.0 copy.14
  105.8 0.6 copy.15
  106.4 0.8 copy.16
Async XLA Ops:
  0.6 1.6 %copy-start = (bf16[1024,1024]{1,0:T(8,128)(2,1)S(1)}, bf16[1024,1024]{1,0:T(8,128)(2,1)}, u32[]{:S(2)}) copy-start(bf16[1024,1024]{1,0:T(8,128)(2,1)} %w_hbm.1) | copy-start | bytes 6291460
  2.2 1.2 %copy-start.1 = (bf16[512,1024]{1,0:T(8,128)(2,1)S(1)}, bf16[512,1024]{1,0:T(8,128)(2,1)}, u32[]{:S(2)}) copy-start(bf16[512,1024]{1,0:T(8,128)(2,1)} %q_hbm.1) | copy-start | bytes 3145732
  3.4 1.0 copy-start.2
  4.5 0.9 copy-start.3
  5.4 0.7 copy-start.4
  6.1 0.7 copy-start.5

commit v2 on v1

v2 whole, which is shorter than its diff:
```python
import math

import jax
import jax.numpy as jnp
from jax import lax
from jax.experimental import pallas as pl
from jax.experimental.pallas import tpu as pltpu
from jax.sharding import PartitionSpec as P

F32 = jnp.float32
BF16 = jnp.bfloat16
MESH = pl.DeviceIdType.MESH
N = 16
HD = 64
TOK = 128
QB = 512
NK = (N + 1) * TOK
TQ = 256
MC = 32
MASKED = -1e30
PAIRS = N // 2
OWN = QB // N
RING = 8
CUT = 2


def to(slot, space):
    return {"slot": slot, "space": space}


def remote(src, dst, send, recv, slot, space):
    return pltpu.make_async_remote_copy(
        src_ref=src, dst_ref=dst, send_sem=send, recv_sem=recv, device_id=to(slot, space), device_id_type=MESH
    )


def wait_bytes(ref, sem):
    pltpu.make_async_copy(ref, ref, sem).wait()


def kernel(
    q_hbm, raw_hbm, pw_ref, old_hbm, valid, w_hbm,
    out, fresh, aged,
    qv, qt, qall, kv, kaug, vt, S, qa, st, sm, ot, lt, sb, rb, ls, lr, mx, mr, att, sel, wv, rawv, halo, xf, zeros,
    lsem, lsem2, lsem3, lsem4, lsem5,
    halo_s, halo_r, kv_s, kv_r, kx_s, kx_r, q_s, q_r, fr_s, fr_r, fx_s, fx_r, ag_s, ag_r,
    res_s, res_r, lse_s, lse_r, mx_s, mx_r, at_s, at_r,
):
    s = lax.axis_index("slot")
    p = lax.axis_index("space")
    half = lax.rem(s, 2)
    rank = s // 2
    partner = s + 1 - 2 * half
    twin = p + 1 - 2 * lax.rem(p, 2)
    lane = lambda shape: lax.broadcasted_iota(jnp.int32, shape, 1)
    line = lambda shape: lax.broadcasted_iota(jnp.int32, shape, 0)

    def head_of(index):
        return old_hbm.at[:, pl.ds(pl.multiple_of(index * TOK, TOK), TOK)]

    q_copy = pltpu.make_async_copy(q_hbm.at[pl.ds(pl.multiple_of(half * TQ, TQ), TQ), :], qv, lsem)
    q_copy.start()
    raw_copy = pltpu.make_async_copy(raw_hbm, rawv, lsem2)
    raw_copy.start()
    kv_copy = pltpu.make_async_copy(head_of(p), kv.at[0, p], lsem3)
    kv_copy.start()
    w_copy = pltpu.make_async_copy(w_hbm, wv, lsem4)
    w_copy.start()

    barrier = pltpu.get_barrier_semaphore()

    def greet(slot, space):
        pl.semaphore_signal(barrier, inc=1, device_id=to(slot, space), device_id_type=MESH)

    for d in range(1, N):
        greet(s, lax.rem(p + d, N))
    for d in range(1, N):
        greet(partner, lax.rem(p + d, N))
    for d in range(1, N):
        greet(lax.rem(s + d, N), p)
    greet(twin, s)
    greet(p, partner)

    @pl.when(s != p)
    def _():
        greet(p, s)

    q_copy.wait()
    for c in range(PAIRS):
        qt[c * 128 : (c + 1) * 128, :] = qv[:, c * 128 : (c + 1) * 128].T

    row_i = line((256, N * HD))
    col_i = lane((256, N * HD))
    sel[...] = jnp.where(row_i % 128 == col_i // HD, 1.0, 0.0).astype(BF16)
    ones_row = jnp.where(line((HD, TQ)) == 0, 1.0, 0.0).astype(BF16)
    for b in range(N):
        qa[b, 3 * HD :, :] = ones_row

    @pl.when(s != p)
    def _():
        pl.semaphore_wait(barrier, 3 * (N - 1) + 3)

    @pl.when(s == p)
    def _():
        pl.semaphore_wait(barrier, 3 * (N - 1) + 2)

    @pl.when(p < N - 1)
    def _():
        remote(raw_hbm.at[:, 1], halo, halo_s, halo_r, s, p + 1).start()

    def move_on(i):
        @pl.when(s < N - 1)
        def _():
            part = pl.ds(i * (TOK // 8), TOK // 8)
            remote(old_hbm.at[part, :], aged.at[part, :], ag_s, ag_r, s + 1, p).start()

    for d in range(1, N):
        peer = lax.rem(p + d, N)
        remote(head_of(peer), kv.at[0, p], kv_s, kv_r, s, peer).start()
        if d % 4 == 0:
            move_on(d // 4 - 1)
    for d in range(1, N):
        peer = lax.rem(p + d, N)
        remote(
            qt.at[pl.ds(pl.multiple_of(peer * HD, HD), HD), :], qall.at[p], q_s, q_r.at[p], s, peer
        ).start()
        if d % 3 == 0:
            move_on(d // 3 + 2)

    for d in range(N):
        peer = lax.rem(p + d, N)
        remote(head_of(peer), kv.at[1, p], kx_s, kx_r, partner, peer).start()

    @pl.when(s == 0)
    def _():
        zeros[...] = jnp.zeros_like(zeros)
        pltpu.make_async_copy(zeros, aged, lsem5).start()

    raw_copy.wait()

    @pl.when(p > 0)
    def _():
        wait_bytes(halo, halo_r)

    @pl.when(p == 0)
    def _():
        halo[...] = jnp.zeros_like(halo)

    edge = jnp.zeros((8, 8, 128), F32)
    for b in range(3):
        xf[b, :, 0:8, :] = edge
        xf[b, :, 8:, :] = (halo[...] if b == 0 else rawv[:, b - 1]).astype(F32)
    weight = pw_ref[...].astype(F32)
    key = lane((MC, 128)) < HD
    for f in range(4):
        total = jnp.zeros((MC, 128), F32)
        for a in range(3):
            frame = 2 * f + a - 1
            if frame < 0:
                continue
            for b in range(3):
                for g in range(3):
                    tap = 9 * a + 3 * b + g
                    total += weight[tap : tap + 1, :] * xf[b, frame, pl.ds(7 + g, MC, stride=2), :]
        mean_lo = jnp.sum(jnp.where(key, total, 0.0), axis=1, keepdims=True) / HD
        mean_hi = jnp.sum(jnp.where(key, 0.0, total), axis=1, keepdims=True) / HD
        centred = total - jnp.where(key, mean_lo, mean_hi)
        square = centred * centred
        var_lo = jnp.sum(jnp.where(key, square, 0.0), axis=1, keepdims=True) / HD
        var_hi = jnp.sum(jnp.where(key, 0.0, square), axis=1, keepdims=True) / HD
        normed = centred * lax.rsqrt(jnp.where(key, var_lo, var_hi) + 1e-06)
        fresh[f * MC : (f + 1) * MC, :] = normed.astype(BF16)

    @pl.when(s != p)
    def _():
        remote(fresh, kv.at[0, N], fr_s, fr_r, p, s).start()

    @pl.when(s == p)
    def _():
        kv[0, N] = fresh[...]

    remote(fresh, kv.at[1, N], fx_s, fx_r, twin, s).start()

    qall[p] = qt[pl.ds(pl.multiple_of(p * HD, HD), HD), :]

    def prepare(k, i, count):
        x = kv[k, i].astype(F32)
        turned = pltpu.roll(x, HD, 1)
        low = lane((TOK, TOK)) < HD
        column = line((TOK, TOK)) % MC
        mask = jnp.where((lane((TOK, TOK)) == HD) & (column >= count), MASKED, 0.0)
        row = pl.ds(pl.multiple_of(i * TOK, TOK), TOK)
        kaug[k, row, 0:128] = jnp.where(low, x, turned).astype(BF16)
        kaug[k, row, 128:256] = jnp.where(low, x, mask).astype(BF16)
        upper = line((TOK, TOK)) < HD
        vt[k, :, row] = jnp.where(upper, 1.0, x.T).astype(BF16)

    def prepare_slot(k, count):
        def one(i, carry):
            prepare(k, i, count)
            return carry

        lax.fori_loop(0, N, one, 0)

    scale = HD ** (-0.5) * math.log2(math.e)
    pair0 = p // 2

    def pair_of(i):
        return lax.rem(pair0 - i + 2 * PAIRS, PAIRS)

    def block_of(i, t):
        return 2 * pair_of(2 * i + t // 2) + t % 2

    def build(b):
        x = qall[b].astype(F32) * scale
        first = x.astype(BF16)
        x = x - first.astype(F32)
        second = x.astype(BF16)
        x = x - second.astype(F32)
        qa[b, 0:HD, :] = first
        qa[b, HD : 2 * HD, :] = second
        qa[b, 2 * HD : 3 * HD, :] = x.astype(BF16)

    def scores(k, b, z):
        peak = None
        for c in range(0, NK, 128):
            block = jnp.dot(kaug[k, c : c + 128, :], qa[b], preferred_element_type=F32)
            S[z, c : c + 128, :] = block
            top = jnp.max(block.reshape(16, 8, TQ), axis=0)
            peak = top if peak is None else jnp.maximum(peak, top)
        return peak

    def weigh(k, z, peak):
        top = jnp.max(peak, axis=0, keepdims=True)
        total = None
        for c in range(0, NK, 256):
            n = min(256, NK - c)
            weights = jnp.exp2(S[z, c : c + n, :] - top).astype(BF16)
            part = jnp.dot(vt[k, :, c : c + n], weights, preferred_element_type=F32)
            total = part if total is None else total + part
        return top, total

    def queries_of(pair):
        wait_bytes(qall.at[0], q_r.at[2 * pair])
        wait_bytes(qall.at[0], q_r.at[2 * pair + 1])

    kv_copy.wait()
    wait_bytes(kv.at[0, pl.ds(0, N - 1)], kv_r)
    prepare_slot(0, valid[s + 1])

    @pl.when(s != p)
    def _():
        wait_bytes(kv.at[0, N], fr_r)

    prepare(0, N, valid[0])
    wait_bytes(qall.at[0], q_r.at[twin])
    queries_of(pair_of(1))
    for t in range(4):
        build(block_of(0, t))
    first_peak = scores(0, block_of(0, 0), 0)

    def own_step(i, peak):
        @pl.when(i < 3)
        def _():
            queries_of(pair_of(2 * i + 2))
            queries_of(pair_of(2 * i + 3))

        for t in range(4):
            b = block_of(i, t)
            build(block_of(i + 1, t))
            later = scores(0, block_of(i, t + 1) if t < 3 else block_of(i + 1, 0), (t + 1) % 2)
            top, total = weigh(0, t % 2, peak)
            st[b] = total
            sm[pl.ds(b, 1), :] = top
            peak = later
        return peak

    lax.fori_loop(0, 4, own_step, first_peak)

    wait_bytes(kv.at[1, pl.ds(0, N)], kx_r)
    prepare_slot(1, valid[partner + 1])
    wait_bytes(kv.at[1, N], fx_r)
    prepare(1, N, valid[0])
    first_peak = scores(1, block_of(0, 0), 0)

    def partner_step(i, peak):
        for t in range(4):
            b = block_of(i, t)
            later = scores(1, block_of(i, t + 1) if t < 3 else block_of(i + 1, 0), (t + 1) % 2)
            top, total = weigh(1, t % 2, peak)
            before = sm[pl.ds(b, 1), :]
            both = jnp.maximum(top, before)
            total = total * jnp.exp2(top - both) + st[b] * jnp.exp2(before - both)
            ot[t // 2, (t % 2) * HD : (t % 2 + 1) * HD, :] = total[HD:, :] / total[:HD, :]
            lt[pl.ds(b, 1), :] = both + jnp.log2(total[0:1, :])
            peak = later
        for u in range(2):
            sb[pair_of(2 * i + u)] = ot[u].T.astype(BF16).reshape(PAIRS, OWN, 128)
        for u in range(2):
            pair = pair_of(2 * i + u)
            for d in range(1, PAIRS):
                owner = lax.rem(rank + d, PAIRS)
                remote(sb.at[pair, owner], rb.at[rank, pair], res_s, res_r, 2 * owner + half, p).start()
        return peak

    lax.fori_loop(0, 4, partner_step, first_peak)

    lse = lt[...]
    first = lse.astype(BF16).astype(F32)
    second = (lse - first).astype(BF16).astype(F32)
    third = lse - first - second
    stacked = jnp.concatenate([first, second, third, jnp.zeros((128 - 3 * N, TQ), F32)], axis=0)
    ls[...] = stacked.T.astype(BF16).reshape(PAIRS, OWN, 128)
    for d in range(1, PAIRS):
        owner = lax.rem(rank + d, PAIRS)
        remote(ls.at[owner], lr.at[rank], lse_s, lse_r, 2 * owner + half, p).start()
    lr[rank] = ls[rank]
    rb[rank] = sb[:, rank]

    wait_bytes(lr.at[pl.ds(0, PAIRS - 1)], lse_r)
    parts = lr[...].astype(F32).reshape(PAIRS * OWN, 128)
    parts = parts + pltpu.roll(parts, 128 - N, 1) + pltpu.roll(parts, 128 - 2 * N, 1)
    parts = jnp.where(lane((PAIRS * OWN, 128)) < N, parts, 0.0).reshape(PAIRS, OWN, 128)
    share = jnp.exp2(parts - jnp.max(parts, axis=0, keepdims=True))
    share = (share / jnp.sum(share, axis=0, keepdims=True)).reshape(PAIRS * OWN, 128)
    share_hi = share.astype(BF16)
    share_lo = (share - share_hi.astype(F32)).astype(BF16)
    shares = jnp.concatenate([share_hi, share_lo], axis=1)
    wait_bytes(rb.at[pl.ds(0, PAIRS - 1)], res_r)
    for j in range(PAIRS):
        spread = jnp.dot(shares, sel[:, j * 128 : (j + 1) * 128], preferred_element_type=F32)
        mixed = jnp.sum(spread.reshape(PAIRS, OWN, 128) * rb[:, j].astype(F32), axis=0)
        mx[j] = mixed.astype(BF16)

    for d in range(1, N):
        peer = lax.rem(p + d, N)
        remote(mx.at[peer // 2], mr.at[p], mx_s, mx_r, s, peer).start()
    mr[p] = mx[p // 2]
    w_copy.wait()
    wait_bytes(mr.at[pl.ds(0, N - 1)], mx_r)
    odd = lax.rem(p, 2) == 1
    left = lane((OWN, 128)) < HD
    pieces = []
    for j in range(PAIRS):
        a = mr[2 * j].astype(F32)
        b = mr[2 * j + 1].astype(F32)
        a = jnp.where(odd, pltpu.roll(a, HD, 1), a)
        b = jnp.where(odd, b, pltpu.roll(b, HD, 1))
        pieces.append(jnp.where(left, a, b).astype(BF16))
    heads = jnp.concatenate(pieces, axis=1)
    att[...] = jnp.dot(heads, wv[...], preferred_element_type=F32).astype(BF16)

    y, z = s // RING, lax.rem(s, RING)
    PART = OWN // CUT

    def start_of(index, c):
        return pl.multiple_of((lax.rem(index, 2) * PAIRS + index // 2) * OWN + c * PART, PART)

    def rows(index, c):
        return out.at[pl.ds(start_of(index, c), PART), :]

    def near(dz):
        return y * RING + lax.rem(z + dz + RING, RING)

    def far(dz):
        return (1 - y) * RING + lax.rem(z + dz + RING, RING)

    sent = [0]

    def push(index, target, c, src=None):
        remote(
            rows(index, c) if src is None else src, rows(index, c), at_s.at[sent[0]], at_r.at[CUT * index + c], target, p
        ).start()
        sent[0] += 1

    def got(index, c):
        wait_bytes(rows(0, 0), at_r.at[CUT * index + c])

    for c in range(CUT):
        push(s, far(0), c, att.at[c * PART : (c + 1) * PART, :])
    for c in range(CUT):
        push(s, near(1), c, att.at[c * PART : (c + 1) * PART, :])
        push(s, near(-1), c, att.at[c * PART : (c + 1) * PART, :])
        out[pl.ds(start_of(s, c), PART), :] = att[c * PART : (c + 1) * PART, :]

    def pass_far(c):
        got(far(0), c)
        push(far(0), near(1), c)
        push(far(0), near(-1), c)

    def pass_near(k, c):
        got(near(-k), c)
        if k < 4:
            push(near(-k), near(1), c)
            got(near(k), c)
        if k < 3:
            push(near(k), near(-1), c)

    def pass_far_on(k, c):
        got(far(k), c)
        if k < 4:
            push(far(k), near(-1), c)
            got(far(-k), c)
        if k < 3:
            push(far(-k), near(1), c)

    for c in range(CUT):
        pass_near(1, c)
    for c in range(CUT):
        pass_far(c)
    for k in range(2, 5):
        for c in range(CUT):
            pass_near(k, c)
        for c in range(CUT):
            pass_far_on(k - 1, c)
    for c in range(CUT):
        pass_far_on(4, c)

    for i in range(sent[0]):
        wait_bytes(rows(0, 0), at_s.at[i])
    wait_bytes(kv.at[0, pl.ds(0, N - 1)], kv_s)
    wait_bytes(kv.at[1, pl.ds(0, N)], kx_s)
    wait_bytes(qall.at[pl.ds(0, N - 1)], q_s)
    wait_bytes(rb.at[pl.ds(0, PAIRS - 1)], res_s)
    wait_bytes(lr.at[pl.ds(0, PAIRS - 1)], lse_s)
    wait_bytes(mr.at[pl.ds(0, N - 1)], mx_s)
    wait_bytes(kv.at[1, N], fx_s)

    @pl.when(p < N - 1)
    def _():
        wait_bytes(halo, halo_s)

    @pl.when(s != p)
    def _():
        wait_bytes(kv.at[0, N], fr_s)

    @pl.when(s < N - 1)
    def _():
        wait_bytes(old_hbm, ag_s)

    @pl.when(s > 0)
    def _():
        wait_bytes(old_hbm, ag_r)

    @pl.when(s == 0)
    def _():
        pltpu.make_async_copy(zeros, aged, lsem5).wait()


def local(queries, raw_clip, pool_weight, old_memory, valid_columns, out_weight):
    dma = pltpu.SemaphoreType.DMA
    anywhere = pl.BlockSpec(memory_space=pl.ANY)
    vmem = pl.BlockSpec(memory_space=pltpu.VMEM)
    attended, fresh, aged = pl.pallas_call(
        kernel,
        out_shape=(
            jax.ShapeDtypeStruct((QB, N * HD), BF16),
            jax.ShapeDtypeStruct((TOK, TOK), BF16),
            jax.ShapeDtypeStruct((TOK, N * TOK), BF16),
        ),
        in_specs=[anywhere, anywhere, vmem, anywhere, pl.BlockSpec(memory_space=pltpu.SMEM), anywhere],
        out_specs=(vmem, vmem, anywhere),
        scratch_shapes=[
            pltpu.VMEM((TQ, N * HD), BF16),
            pltpu.VMEM((N * HD, TQ), BF16),
            pltpu.VMEM((N, HD, TQ), BF16),
            pltpu.VMEM((2, N + 1, TOK, TOK), BF16),
            pltpu.VMEM((2, NK, 256), BF16),
            pltpu.VMEM((2, 128, NK), BF16),
            pltpu.VMEM((2, NK, TQ), F32),
            pltpu.VMEM((N, 256, TQ), BF16),
            pltpu.VMEM((N, 128, TQ), F32),
            pltpu.VMEM((N, TQ), F32),
            pltpu.VMEM((2, 128, TQ), F32),
            pltpu.VMEM((N, TQ), F32),
            pltpu.VMEM((PAIRS, PAIRS, OWN, 128), BF16),
            pltpu.VMEM((PAIRS, PAIRS, OWN, 128), BF16),
            pltpu.VMEM((PAIRS, OWN, 128), BF16),
            pltpu.VMEM((PAIRS, OWN, 128), BF16),
            pltpu.VMEM((PAIRS, OWN, 128), BF16),
            pltpu.VMEM((N, OWN, 128), BF16),
            pltpu.VMEM((OWN, N * HD), BF16),
            pltpu.VMEM((256, N * HD), BF16),
            pltpu.VMEM((N * HD, N * HD), BF16),
            pltpu.VMEM((8, 2, 64, 128), BF16),
            pltpu.VMEM((8, 64, 128), BF16),
            pltpu.VMEM((3, 8, 72, 128), F32),
            pltpu.VMEM((TOK, N * TOK), BF16),
            *[dma] * 5,
            *[dma] * 7,
            dma((N,)),
            *[dma] * 12,
            dma((N * CUT,)),
            dma((N * CUT,)),
        ],
        compiler_params=pltpu.CompilerParams(
            collective_id=0, has_side_effects=True, vmem_limit_bytes=60 * 1024 * 1024
        ),
        name="attend",
    )(
        queries,
        raw_clip,
        pool_weight,
        old_memory.reshape(TOK, N * TOK),
        valid_columns,
        out_weight,
    )
    return (attended, fresh.reshape(4, 1, MC, TOK), aged.reshape(old_memory.shape))


def solution(mesh):
    return jax.shard_map(
        local,
        mesh=mesh,
        in_specs=(
            P("space", None),
            P(None, "space", None, "slot"),
            P(None, "slot"),
            P("slot", None, "space", None, None),
            P(),
            P(),
        ),
        out_specs=(
            P("space", None),
            P(None, "space", None, "slot"),
            P("slot", None, "space", None, None),
        ),
        check_vma=False,
    )
```

time: 109 us -> 99.3 us (0.911)
  local copies, waits for them, and re-layouts: 8.53 us -> 3.74 us
  Pallas kernels: 98 us -> 93.9 us
    unnamed x15 -> x7, local copies, waits for them, and re-layouts: 8.53 us -> 3.74 us
    pallas_call x1, Pallas kernels: 98 us -> 93.9 us  [local(): pl.pallas_call(kernel, out_shape=(jax.ShapeDtypeStruct((QB, N * HD), BF16...]
where the time goes in v2:
time: 99.3 us; the launch traced here: 98.3 us
  Pallas kernels  93.9 us (95%)
  local copies, waits for them, and re-layouts  3.74 us (4%)
    pallas_call x1, Pallas kernels, local(): pl.pallas_call(kernel, out_shape=(jax.ShapeDtypeStruct((QB, N * HD), BF16...  93.9 us
    unnamed x7, local copies, waits for them, and re-layouts  3.74 us

profile of v2, /device:TPU:32, one launch (start us, length us, event | category | flops | bytes accessed | tf_op | source)
XLA Modules:
  0.0 98.3 jit_solution(13133130008097605644)
XLA Ops:
  0.6 93.9 %attend.1 = (bf16[512,1024]{1,0:T(8,128)(2,1)}, bf16[128,128]{1,0:T(8,128)(2,1)}, bf16[128,2048]{1,0:T(8,128)(2,1)}) custom-call(bf16[512,1024]{1,0:T(8,128)(2,1)} %q_hbm.1, bf16[8,2,64,128]{3,2,1,0:T(8,128)(2,1)} %raw_hbm.1, bf16[27,128]{1,0:T(8,128)(2,1)} %pw_ref.1, bf16[128,2048]{1,0:T(8,128)(2,1)} %bitcast.7, s32[17]{0:T(128)} %valid.1, ...), custom_call_target="tpu_custom_call" | custom-call | tf_op jit(solution)/shard_map/attend/pallas_call | solution.py:454
  94.5 0.0 copy-start.1
  94.5 0.0 copy-start
  94.5 2.3 %copy.14 = bf16[512,1024]{1,0:T(8,128)(2,1)} copy(bf16[512,1024]{1,0:T(8,128)(2,1)} %get-tuple-element.15) | data formatting | bytes 2097152
  96.8 0.0 copy-done.1
  96.9 0.6 copy.15
  97.5 0.0 copy-done
  97.5 0.8 copy.16
Async XLA Ops:
  94.5 2.3 %copy-start.1 = (bf16[128,128]{1,0:T(8,128)(2,1)S(1)}, bf16[128,128]{1,0:T(8,128)(2,1)}, u32[]{:S(2)}) copy-start(bf16[128,128]{1,0:T(8,128)(2,1)} %get-tuple-element.7) | copy-start | bytes 98308
  94.5 3.0 %copy-start = (bf16[128,2048]{1,0:T(8,128)(2,1)S(1)}, bf16[128,2048]{1,0:T(8,128)(2,1)}, u32[]{:S(2)}) copy-start(bf16[128,2048]{1,0:T(8,128)(2,1)} %get-tuple-element.8) | copy-start | bytes 1572868

commit v3 on v2

--- a/solution.py
+++ b/solution.py
@@ -14,7 +14,7 @@
 HD = 64
 TOK = 128
 QB = 512
-NK = (N + 1) * TOK
+NK = (N * TOK, (N + 2) * TOK)
 TQ = 256
 MC = 32
 MASKED = -1e30
@@ -41,7 +41,7 @@
 def kernel(
     q_hbm, raw_hbm, pw_ref, old_hbm, valid, w_hbm,
     out, fresh, aged,
-    qv, qt, qall, kv, kaug, vt, S, qa, st, sm, ot, lt, sb, rb, ls, lr, mx, mr, att, sel, wv, rawv, halo, xf, zeros,
+    qv, qt, qall, kv0, kv1, kaug0, kaug1, vt0, vt1, S, qa, st, sm, ot, lt, sb, rb, ls, lr, mx, mr, att, sel, wv, rawv, halo, xf, zeros,
     lsem, lsem2, lsem3, lsem4, lsem5,
     halo_s, halo_r, kv_s, kv_r, kx_s, kx_r, q_s, q_r, fr_s, fr_r, fx_s, fx_r, ag_s, ag_r,
     res_s, res_r, lse_s, lse_r, mx_s, mx_r, at_s, at_r,
@@ -52,6 +52,7 @@
     rank = s // 2
     partner = s + 1 - 2 * half
     twin = p + 1 - 2 * lax.rem(p, 2)
+    kv, kaug, vt = (kv0, kv1), (kaug0, kaug1), (vt0, vt1)
     lane = lambda shape: lax.broadcasted_iota(jnp.int32, shape, 1)
     line = lambda shape: lax.broadcasted_iota(jnp.int32, shape, 0)
 
@@ -62,7 +63,7 @@
     q_copy.start()
     raw_copy = pltpu.make_async_copy(raw_hbm, rawv, lsem2)
     raw_copy.start()
-    kv_copy = pltpu.make_async_copy(head_of(p), kv.at[0, p], lsem3)
+    kv_copy = pltpu.make_async_copy(head_of(p), kv0.at[p], lsem3)
     kv_copy.start()
     w_copy = pltpu.make_async_copy(w_hbm, wv, lsem4)
     w_copy.start()
@@ -74,8 +75,6 @@
 
     for d in range(1, N):
         greet(s, lax.rem(p + d, N))
-    for d in range(1, N):
-        greet(partner, lax.rem(p + d, N))
     for d in range(1, N):
         greet(lax.rem(s + d, N), p)
     greet(twin, s)
@@ -98,38 +97,36 @@
 
     @pl.when(s != p)
     def _():
-        pl.semaphore_wait(barrier, 3 * (N - 1) + 3)
+        pl.semaphore_wait(barrier, 2 * (N - 1) + 3)
 
     @pl.when(s == p)
     def _():
-        pl.semaphore_wait(barrier, 3 * (N - 1) + 2)
+        pl.semaphore_wait(barrier, 2 * (N - 1) + 2)
 
     @pl.when(p < N - 1)
     def _():
         remote(raw_hbm.at[:, 1], halo, halo_s, halo_r, s, p + 1).start()
-
-    def move_on(i):
-        @pl.when(s < N - 1)
-        def _():
-            part = pl.ds(i * (TOK // 8), TOK // 8)
-            remote(old_hbm.at[part, :], aged.at[part, :], ag_s, ag_r, s + 1, p).start()
 
     for d in range(1, N):
         peer = lax.rem(p + d, N)
-        remote(head_of(peer), kv.at[0, p], kv_s, kv_r, s, peer).start()
-        if d % 4 == 0:
-            move_on(d // 4 - 1)
-    for d in range(1, N):
-        peer = lax.rem(p + d, N)
-        remote(
-            qt.at[pl.ds(pl.multiple_of(peer * HD, HD), HD), :], qall.at[p], q_s, q_r.at[p], s, peer
-        ).start()
-        if d % 3 == 0:
-            move_on(d // 3 + 2)
-
-    for d in range(N):
-        peer = lax.rem(p + d, N)
-        remote(head_of(peer), kv.at[1, p], kx_s, kx_r, partner, peer).start()
+        remote(head_of(peer), kv0.at[p], kv_s, kv_r, s, peer).start()
+
+    def ask(peer):
+        remote(qt.at[pl.ds(pl.multiple_of(peer * HD, HD), HD), :], qall.at[p], q_s, q_r.at[p], s, peer).start()
+
+    def ask_pair(k):
+        for b in range(2):
+            ask(2 * lax.rem(p // 2 + k, PAIRS) + b)
+
+    ask(twin)
+    ask_pair(1)
+
+    def move_on():
+        remote(old_hbm, aged, ag_s, ag_r, s + 1, p).start()
+
+    @pl.when((s != RING - 1) & (s < N - 1))
+    def _():
+        move_on()
 
     @pl.when(s == 0)
     def _():
@@ -171,29 +168,19 @@
         normed = centred * lax.rsqrt(jnp.where(key, var_lo, var_hi) + 1e-06)
         fresh[f * MC : (f + 1) * MC, :] = normed.astype(BF16)
 
-    @pl.when(s != p)
-    def _():
-        remote(fresh, kv.at[0, N], fr_s, fr_r, p, s).start()
-
-    @pl.when(s == p)
-    def _():
-        kv[0, N] = fresh[...]
-
-    remote(fresh, kv.at[1, N], fx_s, fx_r, twin, s).start()
-
     qall[p] = qt[pl.ds(pl.multiple_of(p * HD, HD), HD), :]
 
     def prepare(k, i, count):
-        x = kv[k, i].astype(F32)
+        x = kv[k][i].astype(F32)
         turned = pltpu.roll(x, HD, 1)
         low = lane((TOK, TOK)) < HD
         column = line((TOK, TOK)) % MC
         mask = jnp.where((lane((TOK, TOK)) == HD) & (column >= count), MASKED, 0.0)
         row = pl.ds(pl.multiple_of(i * TOK, TOK), TOK)
-        kaug[k, row, 0:128] = jnp.where(low, x, turned).astype(BF16)
-        kaug[k, row, 128:256] = jnp.where(low, x, mask).astype(BF16)
+        kaug[k][row, 0:128] = jnp.where(low, x, turned).astype(BF16)
+        kaug[k][row, 128:256] = jnp.where(low, x, mask).astype(BF16)
         upper = line((TOK, TOK)) < HD
-        vt[k, :, row] = jnp.where(upper, 1.0, x.T).astype(BF16)
+        vt[k][:, row] = jnp.where(upper, 1.0, x.T).astype(BF16)
 
     def prepare_slot(k, count):
         def one(i, carry):
@@ -223,8 +210,8 @@
 
     def scores(k, b, z):
         peak = None
-        for c in range(0, NK, 128):
-            block = jnp.dot(kaug[k, c : c + 128, :], qa[b], preferred_element_type=F32)
+        for c in range(0, NK[k], 128):
+            block = jnp.dot(kaug[k][c : c + 128, :], qa[b], preferred_element_type=F32)
             S[z, c : c + 128, :] = block
             top = jnp.max(block.reshape(16, 8, TQ), axis=0)
             peak = top if peak is None else jnp.maximum(peak, top)
@@ -233,10 +220,9 @@
     def weigh(k, z, peak):
         top = jnp.max(peak, axis=0, keepdims=True)
         total = None
-        for c in range(0, NK, 256):
-            n = min(256, NK - c)
-            weights = jnp.exp2(S[z, c : c + n, :] - top).astype(BF16)
-            part = jnp.dot(vt[k, :, c : c + n], weights, preferred_element_type=F32)
+        for c in range(0, NK[k], 256):
+            weights = jnp.exp2(S[z, c : c + 256, :] - top).astype(BF16)
+            part = jnp.dot(vt[k][:, c : c + 256], weights, preferred_element_type=F32)
             total = part if total is None else total + part
         return top, total
 
@@ -245,14 +231,23 @@
         wait_bytes(qall.at[0], q_r.at[2 * pair + 1])
 
     kv_copy.wait()
-    wait_bytes(kv.at[0, pl.ds(0, N - 1)], kv_r)
+    wait_bytes(kv0.at[pl.ds(0, N - 1)], kv_r)
+
+    remote(kv0, kv1.at[pl.ds(0, N)], kx_s, kx_r, partner, p).start()
+    for k in range(2, PAIRS):
+        ask_pair(k)
+
+    @pl.when(s != p)
+    def _():
+        remote(fresh, kv1.at[N], fr_s, fr_r, p, s).start()
+
+    @pl.when(s == p)
+    def _():
+        kv1[N] = fresh[...]
+
+    remote(fresh, kv1.at[N + 1], fx_s, fx_r, twin, s).start()
+
     prepare_slot(0, valid[s + 1])
-
-    @pl.when(s != p)
-    def _():
-        wait_bytes(kv.at[0, N], fr_r)
-
-    prepare(0, N, valid[0])
     wait_bytes(qall.at[0], q_r.at[twin])
     queries_of(pair_of(1))
     for t in range(4):
@@ -260,6 +255,10 @@
     first_peak = scores(0, block_of(0, 0), 0)
 
     def own_step(i, peak):
+        @pl.when((i == 3) & (s == RING - 1))
+        def _():
+            move_on()
+
         @pl.when(i < 3)
         def _():
             queries_of(pair_of(2 * i + 2))
@@ -277,10 +276,16 @@
 
     lax.fori_loop(0, 4, own_step, first_peak)
 
-    wait_bytes(kv.at[1, pl.ds(0, N)], kx_r)
+    wait_bytes(kv1.at[pl.ds(0, N)], kx_r)
     prepare_slot(1, valid[partner + 1])
-    wait_bytes(kv.at[1, N], fx_r)
+
+    @pl.when(s != p)
+    def _():
+        wait_bytes(kv1.at[N], fr_r)
+
     prepare(1, N, valid[0])
+    wait_bytes(kv1.at[N + 1], fx_r)
+    prepare(1, N + 1, valid[0])
     first_peak = scores(1, block_of(0, 0), 0)
 
     def partner_step(i, peak):
@@ -418,13 +423,13 @@
 
     for i in range(sent[0]):
         wait_bytes(rows(0, 0), at_s.at[i])
-    wait_bytes(kv.at[0, pl.ds(0, N - 1)], kv_s)
-    wait_bytes(kv.at[1, pl.ds(0, N)], kx_s)
+    wait_bytes(kv0.at[pl.ds(0, N - 1)], kv_s)
+    wait_bytes(kv1.at[pl.ds(0, N)], kx_s)
     wait_bytes(qall.at[pl.ds(0, N - 1)], q_s)
     wait_bytes(rb.at[pl.ds(0, PAIRS - 1)], res_s)
     wait_bytes(lr.at[pl.ds(0, PAIRS - 1)], lse_s)
     wait_bytes(mr.at[pl.ds(0, N - 1)], mx_s)
-    wait_bytes(kv.at[1, N], fx_s)
+    wait_bytes(kv1.at[N + 1], fx_s)
 
     @pl.when(p < N - 1)
     def _():
@@ -432,7 +437,7 @@
 
     @pl.when(s != p)
     def _():
-        wait_bytes(kv.at[0, N], fr_s)
+        wait_bytes(kv1.at[N], fr_s)
 
     @pl.when(s < N - 1)
     def _():
@@ -445,6 +450,28 @@
     @pl.when(s == 0)
     def _():
         pltpu.make_async_copy(zeros, aged, lsem5).wait()
+
+
+def settle(a, b, c, a_out, b_out, c_out, a_mid, b_mid, c_mid, ins, outs):
+    moves = []
+    for src, mid, dst, parts in zip((a, c, b), (a_mid, c_mid, b_mid), (a_out, c_out, b_out), (4, 2, 1)):
+        rows = src.shape[0] // parts
+        for i in range(parts):
+            part = pl.ds(i * rows, rows)
+            n = len(moves)
+            moves.append(
+                (
+                    pltpu.make_async_copy(src.at[part, :], mid.at[part, :], ins.at[n]),
+                    pltpu.make_async_copy(mid.at[part, :], dst.at[part, :], outs.at[n]),
+                )
+            )
+    for first, _ in moves:
+        first.start()
+    for first, second in moves:
+        first.wait()
+        second.start()
+    for _, second in moves:
+        second.wait()
 
 
 def local(queries, raw_clip, pool_weight, old_memory, valid_columns, out_weight):
@@ -464,10 +491,13 @@
             pltpu.VMEM((TQ, N * HD), BF16),
             pltpu.VMEM((N * HD, TQ), BF16),
             pltpu.VMEM((N, HD, TQ), BF16),
-            pltpu.VMEM((2, N + 1, TOK, TOK), BF16),
-            pltpu.VMEM((2, NK, 256), BF16),
-            pltpu.VMEM((2, 128, NK), BF16),
-            pltpu.VMEM((2, NK, TQ), F32),
+            pltpu.VMEM((N, TOK, TOK), BF16),
+            pltpu.VMEM((N + 2, TOK, TOK), BF16),
+            pltpu.VMEM((NK[0], 256), BF16),
+            pltpu.VMEM((NK[1], 256), BF16),
+            pltpu.VMEM((128, NK[0]), BF16),
+            pltpu.VMEM((128, NK[1]), BF16),
+            pltpu.VMEM((2, NK[1], TQ), F32),
             pltpu.VMEM((N, 256, TQ), BF16),
             pltpu.VMEM((N, 128, TQ), F32),
             pltpu.VMEM((N, TQ), F32),
@@ -505,6 +535,16 @@
         valid_columns,
         out_weight,
     )
+    shapes = tuple(jax.ShapeDtypeStruct(x.shape, x.dtype) for x in (attended, fresh, aged))
+    attended, fresh, aged = pl.pallas_call(
+        settle,
+        out_shape=shapes,
+        in_specs=[anywhere] * 3,
+        out_specs=(anywhere,) * 3,
+        scratch_shapes=[*(pltpu.VMEM(x.shape, x.dtype) for x in shapes), dma((7,)), dma((7,))],
+        compiler_params=pltpu.CompilerParams(vmem_limit_bytes=60 * 1024 * 1024),
+        name="settle",
+    )(attended, fresh, aged)
     return (attended, fresh.reshape(4, 1, MC, TOK), aged.reshape(old_memory.shape))
 
 

time: 99.3 us -> 88.8 us (0.89)
  the two profiles are of different devices: /device:TPU:32 before, /device:TPU:20 now
where the time goes in v3:
time: 88.8 us; the launch traced here: 88.7 us
  Pallas kernels  88 us (99%)
    pallas_call x1, Pallas kernels, local(): pl.pallas_call(kernel, out_shape=(jax.ShapeDtypeStruct((QB, N * HD), BF16...  85.8 us
    pallas_call x1, Pallas kernels, local(): pl.pallas_call(settle, out_shape=shapes, in_specs=[anywhere] * 3, out_spe...  2.21 us

profile of v3, /device:TPU:20, one launch (start us, length us, event | category | flops | bytes accessed | tf_op | source)
XLA Modules:
  0.0 88.7 jit_solution(15779916647839717990)
XLA Ops:
  0.6 85.8 %attend.1 = (bf16[512,1024]{1,0:T(8,128)(2,1)}, bf16[128,128]{1,0:T(8,128)(2,1)}, bf16[128,2048]{1,0:T(8,128)(2,1)}) custom-call(bf16[512,1024]{1,0:T(8,128)(2,1)} %q_hbm.1, bf16[8,2,64,128]{3,2,1,0:T(8,128)(2,1)} %raw_hbm.1, bf16[27,128]{1,0:T(8,128)(2,1)} %pw_ref.1, bf16[128,2048]{1,0:T(8,128)(2,1)} %bitcast.7, s32[17]{0:T(128)} %valid.1, ...), custom_call_target="tpu_custom_call" | custom-call | tf_op jit(solution)/shard_map/attend/pallas_call | solution.py:481
  86.5 2.2 %settle.1 = (bf16[512,1024]{1,0:T(8,128)(2,1)}, bf16[128,128]{1,0:T(8,128)(2,1)}, bf16[128,2048]{1,0:T(8,128)(2,1)}) custom-call(bf16[512,1024]{1,0:T(8,128)(2,1)} %get-tuple-element.9.a, bf16[128,128]{1,0:T(8,128)(2,1)} %get-tuple-element.10.b, bf16[128,2048]{1,0:T(8,128)(2,1)} %get-tuple-element.11.c), custom_call_target="tpu_custom_call" | custom-call | tf_op jit(solution)/shard_map/settle/pallas_call | solution.py:539

commit v4 on v3

--- a/solution.py
+++ b/solution.py
@@ -20,6 +20,7 @@
 MASKED = -1e30
 PAIRS = N // 2
 OWN = QB // N
+PART = OWN // 2
 RING = 8
 CUT = 2
 
@@ -44,7 +45,7 @@
     qv, qt, qall, kv0, kv1, kaug0, kaug1, vt0, vt1, S, qa, st, sm, ot, lt, sb, rb, ls, lr, mx, mr, att, sel, wv, rawv, halo, xf, zeros,
     lsem, lsem2, lsem3, lsem4, lsem5,
     halo_s, halo_r, kv_s, kv_r, kx_s, kx_r, q_s, q_r, fr_s, fr_r, fx_s, fx_r, ag_s, ag_r,
-    res_s, res_r, lse_s, lse_r, mx_s, mx_r, at_s, at_r,
+    res_s, res_r, lse_s, lse_r, mx_s, mx_r, my_s, my_r, at_s, at_r,
 ):
     s = lax.axis_index("slot")
     p = lax.axis_index("space")
@@ -52,6 +53,8 @@
     rank = s // 2
     partner = s + 1 - 2 * half
     twin = p + 1 - 2 * lax.rem(p, 2)
+    y, z = s // RING, lax.rem(s, RING)
+    across = lax.rem(s + RING, N)
     kv, kaug, vt = (kv0, kv1), (kaug0, kaug1), (vt0, vt1)
     lane = lambda shape: lax.broadcasted_iota(jnp.int32, shape, 1)
     line = lambda shape: lax.broadcasted_iota(jnp.int32, shape, 0)
@@ -76,6 +79,8 @@
     for d in range(1, N):
         greet(s, lax.rem(p + d, N))
     for d in range(1, N):
+        greet(across, lax.rem(p + d, N))
+    for d in range(1, N):
         greet(lax.rem(s + d, N), p)
     greet(twin, s)
     greet(p, partner)
@@ -97,11 +102,11 @@
 
     @pl.when(s != p)
     def _():
-        pl.semaphore_wait(barrier, 2 * (N - 1) + 3)
+        pl.semaphore_wait(barrier, 3 * (N - 1) + 3)
 
     @pl.when(s == p)
     def _():
-        pl.semaphore_wait(barrier, 2 * (N - 1) + 2)
+        pl.semaphore_wait(barrier, 3 * (N - 1) + 2)
 
     @pl.when(p < N - 1)
     def _():
@@ -187,7 +192,7 @@
             prepare(k, i, count)
             return carry
 
-        lax.fori_loop(0, N, one, 0)
+        lax.fori_loop(0, N, one, 0, unroll=4)
 
     scale = HD ** (-0.5) * math.log2(math.e)
     pair0 = p // 2
@@ -199,7 +204,8 @@
         return 2 * pair_of(2 * i + t // 2) + t % 2
 
     def build(b):
-        x = qall[b].astype(F32) * scale
+        x = [qall[2 * (b // 2) + j, :, pl.ds(pl.multiple_of(lax.rem(b, 2) * 128, 128), 128)] for j in range(2)]
+        x = jnp.concatenate(x, axis=1).astype(F32) * scale
         first = x.astype(BF16)
         x = x - first.astype(F32)
         second = x.astype(BF16)
@@ -286,80 +292,98 @@
     prepare(1, N, valid[0])
     wait_bytes(kv1.at[N + 1], fx_r)
     prepare(1, N + 1, valid[0])
-    first_peak = scores(1, block_of(0, 0), 0)
-
-    def partner_step(i, peak):
+    def tile_of(u, k):
+        return 2 * pair_of(k) + u
+
+    def partner_step(u, i, peak):
         for t in range(4):
-            b = block_of(i, t)
-            later = scores(1, block_of(i, t + 1) if t < 3 else block_of(i + 1, 0), (t + 1) % 2)
+            b = tile_of(u, 4 * i + t)
+            if t < 3:
+                following = tile_of(u, 4 * i + t + 1)
+            else:
+                following = tile_of(jnp.minimum(u + (i + 1) // 2, 1), lax.rem(4 * i + 4, PAIRS))
+            later = scores(1, following, (t + 1) % 2)
             top, total = weigh(1, t % 2, peak)
             before = sm[pl.ds(b, 1), :]
             both = jnp.maximum(top, before)
             total = total * jnp.exp2(top - both) + st[b] * jnp.exp2(before - both)
-            ot[t // 2, (t % 2) * HD : (t % 2 + 1) * HD, :] = total[HD:, :] / total[:HD, :]
-            lt[pl.ds(b, 1), :] = both + jnp.log2(total[0:1, :])
+            normed = total[HD:, :] / total[:HD, :]
+            lse = both + jnp.log2(total[0:1, :])
+            for j in range(2):
+                ot[t, j * HD : (j + 1) * HD, :] = normed[:, j * 128 : (j + 1) * 128]
+                lt[u, pl.ds(b - u + j, 1), :] = lse[:, j * 128 : (j + 1) * 128]
             peak = later
-        for u in range(2):
-            sb[pair_of(2 * i + u)] = ot[u].T.astype(BF16).reshape(PAIRS, OWN, 128)
-        for u in range(2):
-            pair = pair_of(2 * i + u)
+        for t in range(4):
+            sb[u, pair_of(4 * i + t)] = ot[t].T.astype(BF16).reshape(PAIRS, PART, 128)
+        for t in range(4):
+            pair = pair_of(4 * i + t)
             for d in range(1, PAIRS):
                 owner = lax.rem(rank + d, PAIRS)
-                remote(sb.at[pair, owner], rb.at[rank, pair], res_s, res_r, 2 * owner + half, p).start()
+                remote(
+                    sb.at[u, pair, owner], rb.at[u, rank, pair], res_s.at[u], res_r.at[u], 2 * owner + half, p
+                ).start()
         return peak
 
-    lax.fori_loop(0, 4, partner_step, first_peak)
-
-    lse = lt[...]
-    first = lse.astype(BF16).astype(F32)
-    second = (lse - first).astype(BF16).astype(F32)
-    third = lse - first - second
-    stacked = jnp.concatenate([first, second, third, jnp.zeros((128 - 3 * N, TQ), F32)], axis=0)
-    ls[...] = stacked.T.astype(BF16).reshape(PAIRS, OWN, 128)
-    for d in range(1, PAIRS):
-        owner = lax.rem(rank + d, PAIRS)
-        remote(ls.at[owner], lr.at[rank], lse_s, lse_r, 2 * owner + half, p).start()
-    lr[rank] = ls[rank]
-    rb[rank] = sb[:, rank]
-
-    wait_bytes(lr.at[pl.ds(0, PAIRS - 1)], lse_r)
-    parts = lr[...].astype(F32).reshape(PAIRS * OWN, 128)
-    parts = parts + pltpu.roll(parts, 128 - N, 1) + pltpu.roll(parts, 128 - 2 * N, 1)
-    parts = jnp.where(lane((PAIRS * OWN, 128)) < N, parts, 0.0).reshape(PAIRS, OWN, 128)
-    share = jnp.exp2(parts - jnp.max(parts, axis=0, keepdims=True))
-    share = (share / jnp.sum(share, axis=0, keepdims=True)).reshape(PAIRS * OWN, 128)
-    share_hi = share.astype(BF16)
-    share_lo = (share - share_hi.astype(F32)).astype(BF16)
-    shares = jnp.concatenate([share_hi, share_lo], axis=1)
-    wait_bytes(rb.at[pl.ds(0, PAIRS - 1)], res_r)
-    for j in range(PAIRS):
-        spread = jnp.dot(shares, sel[:, j * 128 : (j + 1) * 128], preferred_element_type=F32)
-        mixed = jnp.sum(spread.reshape(PAIRS, OWN, 128) * rb[:, j].astype(F32), axis=0)
-        mx[j] = mixed.astype(BF16)
-
-    for d in range(1, N):
-        peer = lax.rem(p + d, N)
-        remote(mx.at[peer // 2], mr.at[p], mx_s, mx_r, s, peer).start()
-    mr[p] = mx[p // 2]
-    w_copy.wait()
-    wait_bytes(mr.at[pl.ds(0, N - 1)], mx_r)
-    odd = lax.rem(p, 2) == 1
-    left = lane((OWN, 128)) < HD
-    pieces = []
-    for j in range(PAIRS):
-        a = mr[2 * j].astype(F32)
-        b = mr[2 * j + 1].astype(F32)
-        a = jnp.where(odd, pltpu.roll(a, HD, 1), a)
-        b = jnp.where(odd, b, pltpu.roll(b, HD, 1))
-        pieces.append(jnp.where(left, a, b).astype(BF16))
-    heads = jnp.concatenate(pieces, axis=1)
-    att[...] = jnp.dot(heads, wv[...], preferred_element_type=F32).astype(BF16)
-
-    y, z = s // RING, lax.rem(s, RING)
-    PART = OWN // CUT
+    def tell(u):
+        lse = lt[u]
+        first = lse.astype(BF16).astype(F32)
+        second = (lse - first).astype(BF16).astype(F32)
+        third = lse - first - second
+        stacked = jnp.concatenate([first, second, third, jnp.zeros((128 - 3 * N, 128), F32)], axis=0)
+        ls[u] = stacked.T.astype(BF16).reshape(PAIRS, PART, 128)
+        for d in range(1, PAIRS):
+            owner = lax.rem(rank + d, PAIRS)
+            remote(ls.at[u, owner], lr.at[u, rank], lse_s.at[u], lse_r.at[u], 2 * owner + half, p).start()
+        lr[u, rank] = ls[u, rank]
+        rb[u, rank] = sb[u, :, rank]
+
+    peak = scores(1, tile_of(0, 0), 0)
+    for u in range(2):
+        peak = lax.fori_loop(0, 2, lambda i, peak, u=u: partner_step(u, i, peak), peak)
+        tell(u)
+
+    def combine(u):
+        wait_bytes(lr.at[u, pl.ds(0, PAIRS - 1)], lse_r.at[u])
+        parts = lr[u].astype(F32).reshape(PAIRS * PART, 128)
+        parts = parts + pltpu.roll(parts, 128 - N, 1) + pltpu.roll(parts, 128 - 2 * N, 1)
+        parts = jnp.where(lane((PAIRS * PART, 128)) < N, parts, 0.0).reshape(PAIRS, PART, 128)
+        share = jnp.exp2(parts - jnp.max(parts, axis=0, keepdims=True))
+        share = (share / jnp.sum(share, axis=0, keepdims=True)).reshape(PAIRS * PART, 128)
+        share_hi = share.astype(BF16)
+        share_lo = (share - share_hi.astype(F32)).astype(BF16)
+        shares = jnp.concatenate([share_hi, share_lo], axis=1)
+        wait_bytes(rb.at[u, pl.ds(0, PAIRS - 1)], res_r.at[u])
+        for j in range(PAIRS):
+            spread = jnp.dot(shares, sel[:, j * 128 : (j + 1) * 128], preferred_element_type=F32)
+            mixed = jnp.sum(spread.reshape(PAIRS, PART, 128) * rb[u, :, j].astype(F32), axis=0)
+            mx[u, j] = mixed.astype(BF16)
+
+        for d in range(1, N):
+            peer = lax.rem(p + d, N)
+            remote(mx.at[u, peer // 2], mr.at[u, 0, p], mx_s.at[u], mx_r.at[u], s, peer).start()
+        for d in range(N):
+            peer = lax.rem(p + d, N)
+            remote(mx.at[u, peer // 2], mr.at[u, 1, p], my_s.at[u], my_r.at[u], across, peer).start()
+        mr[u, 0, p] = mx[u, p // 2]
+
+    def project(u):
+        wait_bytes(mr.at[u, 0, pl.ds(0, N - 1)], mx_r.at[u])
+        wait_bytes(mr.at[u, 1], my_r.at[u])
+        odd = lax.rem(p, 2) == 1
+        left = lane((2 * PART, 128)) < HD
+        pieces = []
+        for j in range(PAIRS):
+            a = mr[u, :, 2 * j].astype(F32).reshape(2 * PART, 128)
+            b = mr[u, :, 2 * j + 1].astype(F32).reshape(2 * PART, 128)
+            a = jnp.where(odd, pltpu.roll(a, HD, 1), a)
+            b = jnp.where(odd, b, pltpu.roll(b, HD, 1))
+            pieces.append(jnp.where(left, a, b).astype(BF16))
+        heads = jnp.concatenate(pieces, axis=1)
+        att[u] = jnp.dot(heads, wv[...], preferred_element_type=F32).astype(BF16)
+
 
     def start_of(index, c):
-        return pl.multiple_of((lax.rem(index, 2) * PAIRS + index // 2) * OWN + c * PART, PART)
+        return pl.multiple_of(lax.rem(index, 2) * TQ + c * 128 + index // 2 * PART, PART)
 
     def rows(index, c):
         return out.at[pl.ds(start_of(index, c), PART), :]
@@ -381,17 +405,12 @@
     def got(index, c):
         wait_bytes(rows(0, 0), at_r.at[CUT * index + c])
 
-    for c in range(CUT):
-        push(s, far(0), c, att.at[c * PART : (c + 1) * PART, :])
-    for c in range(CUT):
-        push(s, near(1), c, att.at[c * PART : (c + 1) * PART, :])
-        push(s, near(-1), c, att.at[c * PART : (c + 1) * PART, :])
-        out[pl.ds(start_of(s, c), PART), :] = att[c * PART : (c + 1) * PART, :]
-
-    def pass_far(c):
-        got(far(0), c)
-        push(far(0), near(1), c)
-        push(far(0), near(-1), c)
+    def begin(c):
+        for i, index in enumerate((s, across)):
+            piece = slice(i * PART, (i + 1) * PART)
+            push(index, near(1), c, att.at[c, piece, :])
+            push(index, near(-1), c, att.at[c, piece, :])
+            out[pl.ds(start_of(index, c), PART), :] = att[c, piece, :]
 
     def pass_near(k, c):
         got(near(-k), c)
@@ -409,26 +428,36 @@
         if k < 3:
             push(far(-k), near(1), c)
 
-    for c in range(CUT):
-        pass_near(1, c)
-    for c in range(CUT):
-        pass_far(c)
-    for k in range(2, 5):
-        for c in range(CUT):
-            pass_near(k, c)
-        for c in range(CUT):
-            pass_far_on(k - 1, c)
-    for c in range(CUT):
-        pass_far_on(4, c)
+    def go_round(k, c):
+        pass_near(k, c)
+        pass_far_on(k, c)
+
+    combine(0)
+    combine(1)
+    w_copy.wait()
+    project(0)
+    begin(0)
+    go_round(1, 0)
+    go_round(2, 0)
+    project(1)
+    begin(1)
+    go_round(1, 1)
+    go_round(3, 0)
+    go_round(2, 1)
+    go_round(4, 0)
+    go_round(3, 1)
+    go_round(4, 1)
 
     for i in range(sent[0]):
         wait_bytes(rows(0, 0), at_s.at[i])
     wait_bytes(kv0.at[pl.ds(0, N - 1)], kv_s)
     wait_bytes(kv1.at[pl.ds(0, N)], kx_s)
     wait_bytes(qall.at[pl.ds(0, N - 1)], q_s)
-    wait_bytes(rb.at[pl.ds(0, PAIRS - 1)], res_s)
-    wait_bytes(lr.at[pl.ds(0, PAIRS - 1)], lse_s)
-    wait_bytes(mr.at[pl.ds(0, N - 1)], mx_s)
+    for u in range(2):
+        wait_bytes(rb.at[u, pl.ds(0, PAIRS - 1)], res_s.at[u])
+        wait_bytes(lr.at[u, pl.ds(0, PAIRS - 1)], lse_s.at[u])
+        wait_bytes(mr.at[u, 0, pl.ds(0, N - 1)], mx_s.at[u])
+        wait_bytes(mr.at[u, 1], my_s.at[u])
     wait_bytes(kv1.at[N + 1], fx_s)
 
     @pl.when(p < N - 1)
@@ -501,15 +530,15 @@
             pltpu.VMEM((N, 256, TQ), BF16),
             pltpu.VMEM((N, 128, TQ), F32),
             pltpu.VMEM((N, TQ), F32),
-            pltpu.VMEM((2, 128, TQ), F32),
-            pltpu.VMEM((N, TQ), F32),
-            pltpu.VMEM((PAIRS, PAIRS, OWN, 128), BF16),
-            pltpu.VMEM((PAIRS, PAIRS, OWN, 128), BF16),
-            pltpu.VMEM((PAIRS, OWN, 128), BF16),
-            pltpu.VMEM((PAIRS, OWN, 128), BF16),
-            pltpu.VMEM((PAIRS, OWN, 128), BF16),
-            pltpu.VMEM((N, OWN, 128), BF16),
-            pltpu.VMEM((OWN, N * HD), BF16),
+            pltpu.VMEM((4, 128, 128), F32),
+            pltpu.VMEM((2, N, 128), F32),
+            pltpu.VMEM((2, PAIRS, PAIRS, PART, 128), BF16),
+            pltpu.VMEM((2, PAIRS, PAIRS, PART, 128), BF16),
+            pltpu.VMEM((2, PAIRS, PART, 128), BF16),
+            pltpu.VMEM((2, PAIRS, PART, 128), BF16),
+            pltpu.VMEM((2, PAIRS, PART, 128), BF16),
+            pltpu.VMEM((2, 2, N, PART, 128), BF16),
+            pltpu.VMEM((2, 2 * PART, N * HD), BF16),
             pltpu.VMEM((256, N * HD), BF16),
             pltpu.VMEM((N * HD, N * HD), BF16),
             pltpu.VMEM((8, 2, 64, 128), BF16),
@@ -519,7 +548,8 @@
             *[dma] * 5,
             *[dma] * 7,
             dma((N,)),
-            *[dma] * 12,
+            *[dma] * 6,
+            *[dma((2,))] * 8,
             dma((N * CUT,)),
             dma((N * CUT,)),
         ],

time: 88.8 us -> 93.8 us (1.056)
  the two profiles are of different devices: /device:TPU:20 before, /device:TPU:32 now
where the time goes in v4:
time: 93.8 us; the launch traced here: 93.6 us
  Pallas kernels  93 us (99%)
    pallas_call x1, Pallas kernels, local(): pl.pallas_call(kernel, out_shape=(jax.ShapeDtypeStruct((QB, N * HD), BF16...  90.8 us
    pallas_call x1, Pallas kernels, local(): pl.pallas_call(settle, out_shape=shapes, in_specs=[anywhere] * 3, out_spe...  2.21 us

profile of v4, /device:TPU:32, one launch (start us, length us, event | category | flops | bytes accessed | tf_op | source)
XLA Modules:
  0.0 93.6 jit_solution(6430963934882461068)
XLA Ops:
  0.6 90.8 %attend.1 = (bf16[512,1024]{1,0:T(8,128)(2,1)}, bf16[128,128]{1,0:T(8,128)(2,1)}, bf16[128,2048]{1,0:T(8,128)(2,1)}) custom-call(bf16[512,1024]{1,0:T(8,128)(2,1)} %q_hbm.1, bf16[8,2,64,128]{3,2,1,0:T(8,128)(2,1)} %raw_hbm.1, bf16[27,128]{1,0:T(8,128)(2,1)} %pw_ref.1, bf16[128,2048]{1,0:T(8,128)(2,1)} %bitcast.7, s32[17]{0:T(128)} %valid.1, ...), custom_call_target="tpu_custom_call" | custom-call | tf_op jit(solution)/shard_map/attend/pallas_call | solution.py:510
  91.4 2.2 %settle.1 = (bf16[512,1024]{1,0:T(8,128)(2,1)}, bf16[128,128]{1,0:T(8,128)(2,1)}, bf16[128,2048]{1,0:T(8,128)(2,1)}) custom-call(bf16[512,1024]{1,0:T(8,128)(2,1)} %get-tuple-element.9.a, bf16[128,128]{1,0:T(8,128)(2,1)} %get-tuple-element.10.b, bf16[128,2048]{1,0:T(8,128)(2,1)} %get-tuple-element.11.c), custom_call_target="tpu_custom_call" | custom-call | tf_op jit(solution)/shard_map/settle/pallas_call | solution.py:569

commit v5 on v3

--- a/solution.py
+++ b/solution.py
@@ -44,7 +44,7 @@
     qv, qt, qall, kv0, kv1, kaug0, kaug1, vt0, vt1, S, qa, st, sm, ot, lt, sb, rb, ls, lr, mx, mr, att, sel, wv, rawv, halo, xf, zeros,
     lsem, lsem2, lsem3, lsem4, lsem5,
     halo_s, halo_r, kv_s, kv_r, kx_s, kx_r, q_s, q_r, fr_s, fr_r, fx_s, fx_r, ag_s, ag_r,
-    res_s, res_r, lse_s, lse_r, mx_s, mx_r, at_s, at_r,
+    res_s, res_r, lse_s, lse_r, mx_s, mx_r, my_s, my_r, at_s, at_r,
 ):
     s = lax.axis_index("slot")
     p = lax.axis_index("space")
@@ -52,6 +52,8 @@
     rank = s // 2
     partner = s + 1 - 2 * half
     twin = p + 1 - 2 * lax.rem(p, 2)
+    y, z = s // RING, lax.rem(s, RING)
+    across = lax.rem(s + RING, N)
     kv, kaug, vt = (kv0, kv1), (kaug0, kaug1), (vt0, vt1)
     lane = lambda shape: lax.broadcasted_iota(jnp.int32, shape, 1)
     line = lambda shape: lax.broadcasted_iota(jnp.int32, shape, 0)
@@ -76,6 +78,8 @@
     for d in range(1, N):
         greet(s, lax.rem(p + d, N))
     for d in range(1, N):
+        greet(across, lax.rem(p + d, N))
+    for d in range(1, N):
         greet(lax.rem(s + d, N), p)
     greet(twin, s)
     greet(p, partner)
@@ -97,11 +101,11 @@
 
     @pl.when(s != p)
     def _():
-        pl.semaphore_wait(barrier, 2 * (N - 1) + 3)
+        pl.semaphore_wait(barrier, 3 * (N - 1) + 3)
 
     @pl.when(s == p)
     def _():
-        pl.semaphore_wait(barrier, 2 * (N - 1) + 2)
+        pl.semaphore_wait(barrier, 3 * (N - 1) + 2)
 
     @pl.when(p < N - 1)
     def _():
@@ -187,7 +191,7 @@
             prepare(k, i, count)
             return carry
 
-        lax.fori_loop(0, N, one, 0)
+        lax.fori_loop(0, N, one, 0, unroll=4)
 
     scale = HD ** (-0.5) * math.log2(math.e)
     pair0 = p // 2
@@ -255,7 +259,7 @@
     first_peak = scores(0, block_of(0, 0), 0)
 
     def own_step(i, peak):
-        @pl.when((i == 3) & (s == RING - 1))
+        @pl.when((i == 1) & (s == RING - 1))
         def _():
             move_on()
 
@@ -339,23 +343,26 @@
 
     for d in range(1, N):
         peer = lax.rem(p + d, N)
-        remote(mx.at[peer // 2], mr.at[p], mx_s, mx_r, s, peer).start()
-    mr[p] = mx[p // 2]
+        remote(mx.at[peer // 2], mr.at[0, p], mx_s, mx_r, s, peer).start()
+    for d in range(N):
+        peer = lax.rem(p + d, N)
+        remote(mx.at[peer // 2], mr.at[1, p], my_s, my_r, across, peer).start()
+    mr[0, p] = mx[p // 2]
     w_copy.wait()
-    wait_bytes(mr.at[pl.ds(0, N - 1)], mx_r)
+    wait_bytes(mr.at[0, pl.ds(0, N - 1)], mx_r)
+    wait_bytes(mr.at[1], my_r)
     odd = lax.rem(p, 2) == 1
-    left = lane((OWN, 128)) < HD
+    left = lane((2 * OWN, 128)) < HD
     pieces = []
     for j in range(PAIRS):
-        a = mr[2 * j].astype(F32)
-        b = mr[2 * j + 1].astype(F32)
+        a = mr[:, 2 * j].astype(F32).reshape(2 * OWN, 128)
+        b = mr[:, 2 * j + 1].astype(F32).reshape(2 * OWN, 128)
         a = jnp.where(odd, pltpu.roll(a, HD, 1), a)
         b = jnp.where(odd, b, pltpu.roll(b, HD, 1))
         pieces.append(jnp.where(left, a, b).astype(BF16))
     heads = jnp.concatenate(pieces, axis=1)
     att[...] = jnp.dot(heads, wv[...], preferred_element_type=F32).astype(BF16)
 
-    y, z = s // RING, lax.rem(s, RING)
     PART = OWN // CUT
 
     def start_of(index, c):
@@ -382,16 +389,11 @@
         wait_bytes(rows(0, 0), at_r.at[CUT * index + c])
 
     for c in range(CUT):
-        push(s, far(0), c, att.at[c * PART : (c + 1) * PART, :])
-    for c in range(CUT):
-        push(s, near(1), c, att.at[c * PART : (c + 1) * PART, :])
-        push(s, near(-1), c, att.at[c * PART : (c + 1) * PART, :])
-        out[pl.ds(start_of(s, c), PART), :] = att[c * PART : (c + 1) * PART, :]
-
-    def pass_far(c):
-        got(far(0), c)
-        push(far(0), near(1), c)
-        push(far(0), near(-1), c)
+        for i, index in enumerate((s, across)):
+            piece = slice(i * OWN + c * PART, i * OWN + (c + 1) * PART)
+            push(index, near(1), c, att.at[piece, :])
+            push(index, near(-1), c, att.at[piece, :])
+            out[pl.ds(start_of(index, c), PART), :] = att[piece, :]
 
     def pass_near(k, c):
         got(near(-k), c)
@@ -409,17 +411,10 @@
         if k < 3:
             push(far(-k), near(1), c)
 
-    for c in range(CUT):
-        pass_near(1, c)
-    for c in range(CUT):
-        pass_far(c)
-    for k in range(2, 5):
+    for k in range(1, 5):
         for c in range(CUT):
             pass_near(k, c)
-        for c in range(CUT):
-            pass_far_on(k - 1, c)
-    for c in range(CUT):
-        pass_far_on(4, c)
+            pass_far_on(k, c)
 
     for i in range(sent[0]):
         wait_bytes(rows(0, 0), at_s.at[i])
@@ -428,7 +423,8 @@
     wait_bytes(qall.at[pl.ds(0, N - 1)], q_s)
     wait_bytes(rb.at[pl.ds(0, PAIRS - 1)], res_s)
     wait_bytes(lr.at[pl.ds(0, PAIRS - 1)], lse_s)
-    wait_bytes(mr.at[pl.ds(0, N - 1)], mx_s)
+    wait_bytes(mr.at[0, pl.ds(0, N - 1)], mx_s)
+    wait_bytes(mr.at[1], my_s)
     wait_bytes(kv1.at[N + 1], fx_s)
 
     @pl.when(p < N - 1)
@@ -508,8 +504,8 @@
             pltpu.VMEM((PAIRS, OWN, 128), BF16),
             pltpu.VMEM((PAIRS, OWN, 128), BF16),
             pltpu.VMEM((PAIRS, OWN, 128), BF16),
-            pltpu.VMEM((N, OWN, 128), BF16),
-            pltpu.VMEM((OWN, N * HD), BF16),
+            pltpu.VMEM((2, N, OWN, 128), BF16),
+            pltpu.VMEM((2 * OWN, N * HD), BF16),
             pltpu.VMEM((256, N * HD), BF16),
             pltpu.VMEM((N * HD, N * HD), BF16),
             pltpu.VMEM((8, 2, 64, 128), BF16),
@@ -519,7 +515,7 @@
             *[dma] * 5,
             *[dma] * 7,
             dma((N,)),
-            *[dma] * 12,
+            *[dma] * 14,
             dma((N * CUT,)),
             dma((N * CUT,)),
         ],

time: 88.8 us -> 85.2 us (0.959)
  the two profiles are of different devices: /device:TPU:20 before, /device:TPU:32 now
where the time goes in v5:
time: 85.2 us; the launch traced here: 85 us
  Pallas kernels  84.4 us (99%)
    pallas_call x1, Pallas kernels, local(): pl.pallas_call(kernel, out_shape=(jax.ShapeDtypeStruct((QB, N * HD), BF16...  82.2 us
    pallas_call x1, Pallas kernels, local(): pl.pallas_call(settle, out_shape=shapes, in_specs=[anywhere] * 3, out_spe...  2.21 us

profile of v5, /device:TPU:32, one launch (start us, length us, event | category | flops | bytes accessed | tf_op | source)
XLA Modules:
  0.0 85.0 jit_solution(13339330905112629055)
XLA Ops:
  0.6 82.2 %attend.1 = (bf16[512,1024]{1,0:T(8,128)(2,1)}, bf16[128,128]{1,0:T(8,128)(2,1)}, bf16[128,2048]{1,0:T(8,128)(2,1)}) custom-call(bf16[512,1024]{1,0:T(8,128)(2,1)} %q_hbm.1, bf16[8,2,64,128]{3,2,1,0:T(8,128)(2,1)} %raw_hbm.1, bf16[27,128]{1,0:T(8,128)(2,1)} %pw_ref.1, bf16[128,2048]{1,0:T(8,128)(2,1)} %bitcast.7, s32[17]{0:T(128)} %valid.1, ...), custom_call_target="tpu_custom_call" | custom-call | tf_op jit(solution)/shard_map/attend/pallas_call | solution.py:477
  82.8 2.2 %settle.1 = (bf16[512,1024]{1,0:T(8,128)(2,1)}, bf16[128,128]{1,0:T(8,128)(2,1)}, bf16[128,2048]{1,0:T(8,128)(2,1)}) custom-call(bf16[512,1024]{1,0:T(8,128)(2,1)} %get-tuple-element.9.a, bf16[128,128]{1,0:T(8,128)(2,1)} %get-tuple-element.10.b, bf16[128,2048]{1,0:T(8,128)(2,1)} %get-tuple-element.11.c), custom_call_target="tpu_custom_call" | custom-call | tf_op jit(solution)/shard_map/settle/pallas_call | solution.py:535
